TPU v7x, 1024 devices: a whole 4x4x32 slice. The times are simulated.
1024 devices in a mesh: lon: 16 (over x, z_hi), lat: 16 (over z_lo, core), dp: 4 (over y).
Axes of the slice: x: 4, y: 4, z: 32 (z_hi: 4, z_lo: 8; z = z_hi * 8 + z_lo), core: 2. Of those that a mesh axis runs over, the one named last changes fastest.
Arguments:
- tokens: bfloat16 [4, 2, 128, 256, 1024], P('dp', None, 'lat', 'lon'), may hold values from -6 to 6
- norm_gain: float32 [1024], replicated, may hold values from 0.1 to 1.9
- w_qkv: bfloat16 [1024, 3072], replicated, may hold values from -8 to 8
- w_out: bfloat16 [1024, 1024], replicated, may hold values from -0.1875 to 0.1875
- obs_vectors: bfloat16 [65536, 1024], P(('lon', 'lat', 'dp')), may hold values from -6 to 6
- obs_lat: int32 [65536, 1], P(('lon', 'lat', 'dp')), may hold values from 0 to 15; in each aligned block of 64 rows (0 to 63, 64 to 127, ...) at most 6 rows name the same one
- obs_cell: int32 [65536], P(('lon', 'lat', 'dp')), may hold values from 0 to 255
- obs_count: int32 [1024], P(('lon', 'lat', 'dp')), may hold values from 1 to 64, 49152 in all
- shift_offsets: int32 [4, 2], P('dp'), may hold values from 1 to 7, as said below
- cotangent: bfloat16 [4, 2, 128, 256, 1024], P('dp', None, 'lat', 'lon'), may hold values from -0.015625 to 0.015625
Outputs:
- block_out: bfloat16 [4, 2, 128, 256, 1024], P('dp', None, 'lat', 'lon')
- gradient: float32 [1024, 1024], P('lon', ('lat', 'dp'))
Inputs may be any that keep to these rules, and one draw needn't show every extreme that they name: `obs_lat`: among the 64 rows of one device at most 6 name the same latitude index; some device has exactly 6 for some index. `obs_count`: some device has exactly 64 live rows. `shift_offsets`: each column takes the value 8 - 1 for some sample.
All inputs are finite; a program needn't handle non-finite values.
Results may differ from a plain program's by a relative error of at most 0.0086.
Values may be sent and summed in bfloat16 or wider, within the bound.
A program may use at most 64 MiB of HBM per device.

v0:
```python
import jax
import jax.numpy as jnp
from jax import lax
from jax.sharding import PartitionSpec as P

HEADS = 16
WIN = 8


def shifted(array, axis, by):
    devices = lax.axis_size(axis)
    return lax.ppermute(array, axis, [(i, (i + by) % devices) for i in range(devices)])


def from_behind(array, axis, by):
    devices = lax.axis_size(axis)
    pairs = [(i, i + by) for i in range(devices) if 0 <= i + by < devices]
    return lax.ppermute(array, axis, pairs)


def to_windows(field_in):
    levels_n, rows_n, cols_n, feat_width = field_in.shape
    blocks = field_in.reshape(levels_n, rows_n // WIN, WIN, cols_n // WIN, WIN, feat_width)
    return blocks.transpose(1, 3, 0, 2, 4, 5).reshape(-1, levels_n * WIN * WIN, feat_width)


def from_windows(windows, levels_n, rows_n, cols_n):
    feat_width = windows.shape[-1]
    blocks = windows.reshape(rows_n // WIN, cols_n // WIN, levels_n, WIN, WIN, feat_width)
    return blocks.transpose(2, 0, 3, 1, 4, 5).reshape(levels_n, rows_n, cols_n, feat_width)


def window_block(win_tokens, win_valid, norm_gain, w_qkv, w_out):
    n_win, n_tok, d_model = win_tokens.shape
    head_dim = d_model // HEADS
    as_float = win_tokens.astype(jnp.float32)
    average = jnp.mean(as_float, axis=-1, keepdims=True)
    centred = as_float - average
    variance = jnp.mean(centred * centred, axis=-1, keepdims=True)
    normed = (centred * lax.rsqrt(variance + 1e-05) * norm_gain).astype(jnp.bfloat16)
    projected = jnp.dot(
        normed.reshape(-1, d_model), w_qkv, preferred_element_type=jnp.float32
    ).astype(jnp.bfloat16)
    projected = projected.reshape(n_win, n_tok, 3, HEADS, head_dim)
    queries = projected[:, :, 0]
    key_rows = projected[:, :, 1]
    values = projected[:, :, 2]
    scores = jnp.einsum(
        "wqhd,wkhd->whqk", queries, key_rows, preferred_element_type=jnp.float32
    ) * head_dim ** (-0.5)
    scores = jnp.where(win_valid[:, None, None, :], scores, -1e30)
    highest = jnp.max(scores, axis=-1, keepdims=True)
    powers = jnp.exp(scores - highest)
    weights = (powers / jnp.sum(powers, axis=-1, keepdims=True)).astype(jnp.bfloat16)
    context = jnp.einsum(
        "whqk,wkhd->wqhd", weights, values, preferred_element_type=jnp.float32
    ).astype(jnp.bfloat16)
    context = context.reshape(n_win, n_tok, d_model)
    result = jnp.dot(context.reshape(-1, d_model), w_out, preferred_element_type=jnp.float32)
    return ((as_float + result.reshape(n_win, n_tok, d_model)).astype(jnp.bfloat16), context)


def on_device(
    tokens,
    norm_gain,
    w_qkv,
    w_out,
    obs_vectors,
    obs_lat,
    obs_cell,
    obs_count,
    shift_offsets,
    cotangent,
):
    n_batch, levels, lat_dev, lon_dev, d_model = tokens.shape
    n_lat = lax.axis_size("lat")
    obs_rows = obs_vectors.shape[0]
    capacity = obs_rows * 3 // (2 * n_lat)
    n_slots = n_lat * capacity
    destination = obs_lat[:, 0]
    one_hot = (destination[:, None] == jnp.arange(n_lat, dtype=jnp.int32)[None, :]).astype(
        jnp.int32
    )
    earlier = jnp.cumsum(one_hot, axis=0) - one_hot
    rank_in = jnp.sum(earlier * one_hot, axis=1)
    slot_of = destination * capacity + rank_in
    is_live = jnp.arange(obs_rows, dtype=jnp.int32) < obs_count[0]
    cell_tag = jnp.where(is_live, obs_cell, -1)
    chooser = slot_of[None, :] == jnp.arange(n_slots, dtype=jnp.int32)[:, None]
    sent_rows = (
        jnp.dot(chooser.astype(jnp.bfloat16), obs_vectors, preferred_element_type=jnp.float32)
        .astype(jnp.bfloat16)
        .reshape(n_lat, capacity, d_model)
    )
    sent_tags = (jnp.sum(chooser.astype(jnp.int32) * (cell_tag[None, :] + 1), axis=1) - 1).reshape(
        n_lat, capacity
    )
    got_rows, got_tags = (
        lax.all_to_all(sent_rows, "lat", split_axis=0, concat_axis=0, tiled=True),
        lax.all_to_all(sent_tags, "lat", split_axis=0, concat_axis=0, tiled=True),
    )
    flat_tokens = tokens.reshape(-1, d_model)
    placer = (
        got_tags.reshape(-1)[None, :] == jnp.arange(flat_tokens.shape[0], dtype=jnp.int32)[:, None]
    ).astype(jnp.bfloat16)
    added = jnp.dot(placer, got_rows.reshape(-1, d_model), preferred_element_type=jnp.float32)
    enriched = (flat_tokens.astype(jnp.float32) + added).astype(jnp.bfloat16).reshape(tokens.shape)
    margin = WIN - 1
    east_cols = shifted(enriched[:, :, :, :margin], "lon", -1)
    widened = jnp.concatenate([enriched, east_cols], axis=3)
    north_part = from_behind(widened[:, :, :margin], "lat", -1)
    extended = jnp.concatenate([widened, north_part], axis=2)
    lat_shift = shift_offsets[0, 0]
    lon_shift = shift_offsets[0, 1]
    anchor = jnp.zeros((), jnp.int32)
    region = lax.dynamic_slice(
        extended, (anchor, anchor, lat_shift, lon_shift, anchor), tokens.shape
    )[0]
    source_rows = lax.axis_index("lat") * lat_dev + lat_shift + jnp.arange(lat_dev, dtype=jnp.int32)
    is_valid = jnp.broadcast_to(
        (source_rows < lat_dev * n_lat)[None, :, None, None], (levels, lat_dev, lon_dev, 1)
    )
    mixed, context = window_block(
        to_windows(region), to_windows(is_valid)[..., 0], norm_gain, w_qkv, w_out
    )
    block_out = from_windows(mixed, levels, lat_dev, lon_dev)[None]
    cot_rows = to_windows(cotangent[0]).reshape(-1, d_model)
    context_rows = context.reshape(-1, d_model)
    contract = (((0,), (0,)), ((), ()))
    partial_rows = lax.psum_scatter(
        lax.dot_general(cot_rows, context_rows, contract, preferred_element_type=jnp.float32),
        "lon",
        scatter_dimension=0,
        tiled=True,
    )
    gradient = lax.psum_scatter(partial_rows, ("lat", "dp"), scatter_dimension=1, tiled=True)
    return (block_out, gradient)


def solution(mesh):
    placed = (
        P("dp", None, "lat", "lon", None),
        P(),
        P(),
        P(),
        P(("lon", "lat", "dp"), None),
        P(("lon", "lat", "dp"), None),
        P(("lon", "lat", "dp")),
        P(("lon", "lat", "dp")),
        P("dp", None),
        P("dp", None, "lat", "lon", None),
    )
    return jax.shard_map(
        on_device,
        mesh=mesh,
        in_specs=placed,
        out_specs=(P("dp", None, "lat", "lon", None), P("lon", ("lat", "dp"))),
        check_vma=False,
    )
```

profile of v0, /device:TPU:1, one launch (start us, length us, event | category | flops | bytes accessed | tf_op | source)
XLA Modules:
  0.0 871.9 jit_solution(17361416427382308828)
XLA Ops:
  7.2 0.0 copy-start
  7.2 0.0 copy-start.3
  8.0 0.7 fusion.35
  8.7 0.1 reduce_window_sum.11
  8.8 0.8 select_reduce_fusion.1
  9.7 0.7 fusion.37
  10.3 0.1 select_reduce_fusion
  10.4 0.7 sub.33
  11.1 17.4 %all-to-all-start = ((s32[16,1,6]{2,1,0:T(1,128)}), s32[16,1,6]{2,1,0:T(1,128)S(1)}, u32[]{:S(2)}, u32[]{:S(2)}) async-start(s32[16,1,6]{2,1,0:T(1,128)} %bitcast.3), calls=%async_computation | async-start | bytes 16384 | tf_op jit(solution)/shard_map/all_to_all | solution.py:100
  28.5 1.2 convolution_convert_fusion.2
  29.7 0.8 reshape.111
  30.5 7.7 all-to-all-done
  38.2 4.0 all-to-all-start.1
  42.3 0.0 reduce-scatter.7.cloned.1.call-start
  42.3 0.5 broadcast.90
  42.9 0.7 reduce.5
  43.5 0.1 eq.47
  43.6 15.8 %all-to-all-done.1 = bf16[16,6,1024]{2,1,0:T(8,128)(2,1)S(1)} async-done(((bf16[16,6,1024]{2,1,0:T(8,128)(2,1)}), bf16[16,6,1024]{2,1,0:T(8,128)(2,1)S(1)}, u32[]{:S(2)}, u32[]{:S(2)}) %all-to-all-start.1) | async-done | bytes 196640 | tf_op jit(solution)/shard_map/all_to_all | solution.py:99
  59.4 0.1 reshape.112
  59.4 0.0 copy-done.3
  59.5 0.3 fusion.7
  59.7 0.0 copy-start.5
  59.8 0.3 copy.82
  60.0 14.0 %collective-permute-start = (bf16[1,2,8,7,1024]{4,1,3,2,0:T(2,128)(2,1)S(1)}, bf16[1,2,8,7,1024]{4,1,3,2,0:T(2,128)(2,1)S(1)}, u32[]{:S(2)}, u32[]{:S(2)}) collective-permute-start(bf16[1,2,8,7,1024]{4,1,3,2,0:T(2,128)(2,1)S(1)} %copy.82), channel_id=1, source_target_pairs={{0,960},{64,0},{128,64},{192,128},{256,192},{320,256},{384,320},{4... | collective-permute-start | bytes 688136 | tf_op jit(solution)/shard_map/ppermute | solution.py:12
  74.0 0.5 constant_dynamic-update-slice_fusion.1
  74.6 29.5 %collective-permute-done = bf16[1,2,8,7,1024]{4,1,3,2,0:T(2,128)(2,1)S(1)} collective-permute-done((bf16[1,2,8,7,1024]{4,1,3,2,0:T(2,128)(2,1)S(1)}, bf16[1,2,8,7,1024]{4,1,3,2,0:T(2,128)(2,1)S(1)}, u32[]{:S(2)}, u32[]{:S(2)}) %collective-permute-start) | collective-permute-done | bytes 229408 | tf_op jit(solution)/shard_map/ppermute | solution.py:12
  104.1 0.2 constant_dynamic-update-slice_fusion
  104.3 1.3 slice.29
  105.6 2.1 collective-permute-start.1
  107.7 0.6 fusion.45
  111.6 0.1 transpose.43
  111.7 0.1 transpose.44
  111.8 1.9 copy.63
  114.9 5.4 collective-permute-done.1
  120.4 1.3 fusion.19
  121.7 0.1 copy.54
  121.8 0.0 copy-start.4
  121.8 0.4 convert.10
  122.3 0.4 bitcast_reduce_fusion
  122.6 0.4 fusion.15
  123.0 0.1 div.17
  123.1 0.1 rsqrt.12
  123.2 0.2 fusion.13
  123.4 5.7 convolution_convert_fusion
  129.2 4.9 reshape.125
  134.0 3.8 fusion.44
  137.8 2.8 copy.70
  140.6 2.8 copy.71
  143.4 2.8 copy.72
  146.1 3.4 fusion.46
  149.6 2.2 convolution_convert_fusion.1
  151.8 0.0 copy-start.2
  151.8 0.8 copy-done.2
  152.6 0.5 copy.62
  153.2 2.7 convolution_bitcast_fusion
  155.8 5.3 copy.66
  161.2 0.0 reduce-scatter.7.cloned.1.call-update
  161.2 0.0 reduce-scatter.5.cloned.1.call-start
  161.3 271.4 %reduce-scatter.7.cloned.1.call-done = f32[64,1024]{1,0:T(8,128)} async-done(((f32[1024,1024]{1,0:T(8,128)}), f32[64,1024]{1,0:T(8,128)}) %reduce-scatter.7.cloned.1.call-update) | async-done | bytes 262160
  432.7 1.9 copy.67
  434.6 0.0 reduce-scatter.5.cloned.1.call-update
  434.6 1.8 fusion.8
  436.4 0.8 copy.83
  437.2 427.8 %reduce-scatter.5.cloned.1.call-done = f32[64,16]{0,1:T(8,128)} async-done(((f32[64,1024]{0,1:T(8,128)}), f32[64,16]{0,1:T(8,128)}) %reduce-scatter.5.cloned.1.call-update) | async-done | bytes 4112 | tf_op jit(solution)/shard_map/reduce_scatter | solution.py:136
  (10 shorter events, 0.1 us)
Async XLA Ops:
  7.2 427.5 %copy-start = (bf16[1024,1024]{1,0:T(8,128)(2,1)S(1)}, bf16[1024,1024]{1,0:T(8,128)(2,1)}, u32[]{:S(2)}) copy-start(bf16[1024,1024]{1,0:T(8,128)(2,1)} %param.13) | copy-start | bytes 6291460
  7.2 52.3 %copy-start.3 = (bf16[1,2,8,16,1024]{4,3,2,1,0:T(8,128)(2,1)S(1)}, bf16[1,2,8,16,1024]{4,3,2,1,0:T(8,128)(2,1)}, u32[]{:S(2)}) copy-start(bf16[1,2,8,16,1024]{4,3,2,1,0:T(8,128)(2,1)} %param.10) | copy-start | bytes 1572868
  11.1 27.1 %all-to-all-start = ((s32[16,1,6]{2,1,0:T(1,128)}), s32[16,1,6]{2,1,0:T(1,128)S(1)}, u32[]{:S(2)}, u32[]{:S(2)}) async-start(s32[16,1,6]{2,1,0:T(1,128)} %bitcast.3), calls=%async_computation | async-start | bytes 16384 | tf_op jit(solution)/shard_map/all_to_all | solution.py:100
  38.2 21.1 %all-to-all-start.1 = ((bf16[16,6,1024]{2,1,0:T(8,128)(2,1)}), bf16[16,6,1024]{2,1,0:T(8,128)(2,1)S(1)}, u32[]{:S(2)}, u32[]{:S(2)}) async-start(bf16[16,6,1024]{2,1,0:T(8,128)(2,1)} %reshape.111), calls=%async_computation.1 | async-start | bytes 524288 | tf_op jit(solution)/shard_map/all_to_all | solution.py:99
  42.3 390.4 %reduce-scatter.7.cloned.1.call-start = ((), (), s32[]{:S(2)}) async-start(), calls=%async_computation.5 | async-start | bytes 4456448
  59.7 48.0 %copy-start.5 = (s32[1,2]{1,0:T(1,128)S(1)}, s32[1,2]{1,0:T(1,128)}, u32[]{:S(2)}) copy-start(s32[1,2]{1,0:T(1,128)} %param.18) | copy-start | bytes 28
  60.0 44.1 %collective-permute-start = (bf16[1,2,8,7,1024]{4,1,3,2,0:T(2,128)(2,1)S(1)}, bf16[1,2,8,7,1024]{4,1,3,2,0:T(2,128)(2,1)S(1)}, u32[]{:S(2)}, u32[]{:S(2)}) collective-permute-start(bf16[1,2,8,7,1024]{4,1,3,2,0:T(2,128)(2,1)S(1)} %copy.82), channel_id=1, source_target_pairs={{0,960},{64,0},{128,64},{192,128},{256,192},{320,256},{384,320},{4... | collective-permute-start | bytes 688136 | tf_op jit(solution)/shard_map/ppermute | solution.py:12
  105.6 14.8 %collective-permute-start.1 = (bf16[1,2,7,23,1024]{4,1,3,2,0:T(2,128)(2,1)}, bf16[1,2,7,23,1024]{4,1,3,2,0:T(2,128)(2,1)S(1)}, u32[]{:S(2)}, u32[]{:S(2)}) collective-permute-start(bf16[1,2,7,23,1024]{4,1,3,2,0:T(2,128)(2,1)} %slice.29), channel_id=1, source_target_pairs={{4,0},{8,4},{12,8},{16,12},{20,16},{24,20},{28,24},{32,28},{36,32}... | collective-permute-start | bytes 1978376 | tf_op jit(solution)/shard_map/ppermute | solution.py:18
  121.8 1.4 copy-start.4
  149.6 3.6 copy-start.1
  151.8 0.8 copy-start.2
  161.2 703.9 %reduce-scatter.5.cloned.1.call-start = ((), (), s32[]{:S(2)}) async-start(), calls=%async_computation.4 | async-start | bytes 532480 | tf_op jit(solution)/shard_map/reduce_scatter | solution.py:136
Sparse Core Ops, SparseCore 0:
  161.3 271.2 reduce-scatter.6
  436.6 428.4 reduce-scatter.4
where the time goes:
time: 887 us; the launch traced here: 872 us
  waiting for transfers between devices  758 us (85%)
  starting transfers between devices  37.6 us (4%)
  local copies, waits for them, and re-layouts  33.8 us (4%)
  between operations  19.6 us (2%)
  matrix products  17.3 us (2%)
    reduce_scatter x1, waiting for transfers between devices, on_device(): lax.psum_scatter(partial_rows, ('lat', 'dp'), scatter_dimension=1, tiled=...  428 us
    unnamed x3, waiting for transfers between devices  271 us
    ppermute x1, waiting for transfers between devices, shifted(): lax.ppermute(array, axis, [(i, (i + by) % devices) for i in range(devices)])  29.5 us
  transfers between devices with their start and end apart: 6, of which 6 were waited for; matrix products, arithmetic and copies ran while one was open for 1% of the time, Pallas kernels for 0%

commit v1 on v0

v1 whole, which is shorter than its diff:
```python
import functools

import jax
import jax.numpy as jnp
from jax import lax
from jax.experimental import pallas as pl
from jax.experimental.pallas import tpu as pltpu
from jax.sharding import PartitionSpec as P

HEADS = 16
WIN = 8
MESH = pl.DeviceIdType.MESH


def shifted(array, axis, by):
    devices = lax.axis_size(axis)
    return lax.ppermute(array, axis, [(i, (i + by) % devices) for i in range(devices)])


def from_behind(array, axis, by):
    devices = lax.axis_size(axis)
    pairs = [(i, i + by) for i in range(devices) if 0 <= i + by < devices]
    return lax.ppermute(array, axis, pairs)


def block_kernel(
    base_ref, region_ref, gain_ref, w_qkv_ref, w_out_ref, cot_ref, out_ref, g_ref, qkv_ref, ctx_ref, ctx_t_ref
):
    n_tok, d_model = region_ref.shape
    head_dim = d_model // HEADS
    pair = 2 * head_dim
    groups = n_tok // (2 * WIN)
    win_tok = n_tok // 2
    as_float = region_ref[...].astype(jnp.float32)
    average = jnp.mean(as_float, axis=-1, keepdims=True)
    centred = as_float - average
    variance = jnp.mean(centred * centred, axis=-1, keepdims=True)
    normed = (centred * lax.rsqrt(variance + 1e-05) * gain_ref[...]).astype(jnp.bfloat16)
    block = 512
    for col in range(0, 3 * d_model, block):
        part = jnp.dot(normed, w_qkv_ref[:, col : col + block], preferred_element_type=jnp.float32)
        part = part.reshape(groups, 2, WIN, block)
        for win in range(2):
            qkv_ref[win, :, col : col + block] = part[:, win].reshape(win_tok, block).astype(jnp.bfloat16)
    lane = lax.broadcasted_iota(jnp.int32, (win_tok, pair), 1)
    first = lane < head_dim
    key = lax.broadcasted_iota(jnp.int32, (win_tok, 2 * win_tok), 1)
    is_valid = base_ref[0] + (key // WIN) % WIN < base_ref[1]
    for win in range(2):
        for two in range(HEADS // 2):
            at = two * pair
            queries = qkv_ref[win, :, at : at + pair]
            keys = qkv_ref[win, :, d_model + at : d_model + at + pair]
            values = qkv_ref[win, :, 2 * d_model + at : 2 * d_model + at + pair]
            zero = jnp.zeros_like(keys)
            keys = jnp.concatenate([jnp.where(first, keys, zero), jnp.where(first, zero, keys)], axis=0)
            values = jnp.concatenate([jnp.where(first, values, zero), jnp.where(first, zero, values)], axis=0)
            scores = lax.dot_general(
                queries, keys, (((1,), (1,)), ((), ())), preferred_element_type=jnp.float32
            ) * head_dim ** (-0.5)
            scores = jnp.where(is_valid, scores, -1e30)
            weights = []
            for half in range(2):
                mine = scores[:, half * win_tok : (half + 1) * win_tok]
                powers = jnp.exp(mine - jnp.max(mine, axis=-1, keepdims=True))
                weights.append((powers / jnp.sum(powers, axis=-1, keepdims=True)).astype(jnp.bfloat16))
            context = jnp.dot(jnp.concatenate(weights, axis=1), values, preferred_element_type=jnp.float32)
            ctx_ref[:, win, :, at : at + pair] = context.reshape(groups, WIN, pair)
    context = ctx_ref[...].reshape(n_tok, d_model).astype(jnp.bfloat16)
    for col in range(0, d_model, block):
        result = jnp.dot(context, w_out_ref[:, col : col + block], preferred_element_type=jnp.float32)
        out_ref[:, col : col + block] = (
            region_ref[:, col : col + block].astype(jnp.float32) + result
        ).astype(jnp.bfloat16)
    ctx_t_ref[...] = context.T
    cores, n_x, n_y, rows, wide = g_ref.shape
    n_z = rows // 16
    for x in range(n_x):
        part = jnp.dot(
            ctx_t_ref[...], cot_ref[:, x * wide : (x + 1) * wide], preferred_element_type=jnp.float32
        ).astype(jnp.bfloat16)
        for z in range(n_z):
            for core in range(cores):
                for y in range(n_y):
                    at = ((z * cores + core) * n_y + y) * 16
                    g_ref[core, x, y, z * 16 : (z + 1) * 16, :] = part[at : at + 16, :]


def run_block(base, region, gain, w_qkv, w_out, cot, dims):
    n_tok, d_model = region.shape
    vmem = pl.BlockSpec(memory_space=pltpu.VMEM)
    return pl.pallas_call(
        block_kernel,
        out_shape=(
            jax.ShapeDtypeStruct((n_tok, d_model), jnp.bfloat16),
            jax.ShapeDtypeStruct(dims, jnp.bfloat16),
        ),
        in_specs=[pl.BlockSpec(memory_space=pltpu.SMEM)] + [vmem] * 5,
        out_specs=(vmem, vmem),
        scratch_shapes=[
            pltpu.VMEM((2, n_tok // 2, 3 * d_model), jnp.bfloat16),
            pltpu.VMEM((n_tok // (2 * WIN), 2, WIN, d_model), jnp.float32),
            pltpu.VMEM((d_model, n_tok), jnp.bfloat16),
        ],
        compiler_params=pltpu.CompilerParams(vmem_limit_bytes=40 << 20),
        cost_estimate=pl.CostEstimate(flops=3 << 30, bytes_accessed=12 << 20, transcendentals=1 << 19),
        name="block",
    )(base, region, gain, w_qkv, w_out, cot)


def reduce_kernel(
    n_x, n_y, n_h, n_l,
    g_ref, out_ref,
    c_recv, x_send, x_recv, x_sum, y_send, y_recv, l_send, l_recv, h_send, h_recv,
    c_sems, x_sems, y_sems, l_sems, h_sems,
):
    lon, lat, y = lax.axis_index("lon"), lax.axis_index("lat"), lax.axis_index("dp")
    x, z_hi = lon // n_h, lon % n_h
    z_lo, core = lat // 2, lat % 2
    f32, bf16 = jnp.float32, jnp.bfloat16

    def at_x(k):
        return {"lon": ((x + k) % n_x) * n_h + z_hi}

    def at_y(k):
        return {"dp": (y + k) % n_y}

    def at_l(k):
        return {"lat": ((z_lo + k) % n_l) * 2 + core}

    def at_h(other):
        return {"lon": x * n_h + other}

    pal = {"lat": z_lo * 2 + 1 - core}
    near = z_hi + 1 - 2 * (z_hi % 2)
    far = (z_hi + n_h - 1 + 2 * (z_hi % 2)) % n_h
    peers = [pal] + [at_x(k) for k in range(1, n_x)] + [at_y(k) for k in range(1, n_y)]
    peers += [at_l(k) for k in range(1, n_l)] + [at_h(near), at_h(far)]
    barrier = pltpu.get_barrier_semaphore()
    for peer in peers:
        pl.semaphore_signal(barrier, inc=1, device_id=peer, device_id_type=MESH)
    pl.semaphore_wait(barrier, len(peers))

    def copy(src, dst, sems, k, where):
        return pltpu.make_async_remote_copy(
            src_ref=src, dst_ref=dst, send_sem=sems.at[0, k], recv_sem=sems.at[1, k],
            device_id=where, device_id_type=MESH,
        )

    order = [2, 1, 3, 0] if n_x == 4 else [k for k in range(1, n_x)] + [0]
    c_copies = {}
    for k in order:
        dest = (x + k) % n_x
        c_copies[k] = copy(g_ref.at[1 - core, dest], c_recv.at[k], c_sems, k, pal)
        c_copies[k].start()
    x_copies = {}
    for k in order:
        dest = (x + k) % n_x
        c_copies[k].wait_recv()
        for i in range(n_y):
            part = g_ref[core, dest, i].astype(f32) + c_recv[k, i].astype(f32)
            if k:
                x_send[k - 1, i] = part.astype(bf16)
            else:
                x_sum[i] = part
        if k:
            x_copies[k] = copy(x_send.at[k - 1], x_recv.at[k - 1], x_sems, k - 1, at_x(k))
            x_copies[k].start()
    for k in range(1, n_x):
        x_copies[k].wait_recv()
    y_copies = {}
    for k in list(range(1, n_y)) + [0]:
        dest = (y + k) % n_y
        part = x_sum[dest]
        for j in range(n_x - 1):
            part = part + x_recv[j, dest].astype(f32)
        if k:
            y_send[k - 1] = part.astype(bf16)
            y_copies[k] = copy(y_send.at[k - 1], y_recv.at[k - 1], y_sems, k - 1, at_y(k))
            y_copies[k].start()
    for k in range(1, n_y):
        y_copies[k].wait_recv()
        part = part + y_recv[k - 1].astype(f32)
    rows, wide = part.shape
    l_send[...] = part.reshape(n_l, rows // n_l, wide).astype(bf16)
    x_sum[0] = part
    l_copies = {}
    for k in range(1, n_l):
        l_copies[k] = copy(l_send.at[(z_lo + k) % n_l], l_recv.at[k - 1], l_sems, k - 1, at_l(k))
        l_copies[k].start()
    part = x_sum[0, pl.ds(pl.multiple_of(z_lo * (rows // n_l), rows // n_l), rows // n_l), :]
    for k in range(1, n_l):
        l_copies[k].wait_recv()
        part = part + l_recv[k - 1].astype(f32)
    h_send[0] = part
    first = copy(h_send.at[0], h_recv.at[0], h_sems, 0, at_h(near))
    first.start()
    first.wait_recv()
    part = part + h_recv[0]
    h_send[1] = part
    second = copy(h_send.at[1], h_recv.at[1], h_sems, 1, at_h(far))
    second.start()
    second.wait_recv()
    out_ref[...] = part + h_recv[1]
    for group in (c_copies, x_copies, y_copies, l_copies):
        for k in group:
            group[k].wait_send()
    first.wait_send()
    second.wait_send()


def run_reduce(g, n_h):
    _, n_x, n_y, rows, wide = g.shape
    n_l = rows // 16
    vmem = pl.BlockSpec(memory_space=pltpu.VMEM)
    bf16, f32 = jnp.bfloat16, jnp.float32
    return pl.pallas_call(
        functools.partial(reduce_kernel, n_x, n_y, n_h, n_l),
        out_shape=jax.ShapeDtypeStruct((16, wide), f32),
        in_specs=[vmem],
        out_specs=vmem,
        scratch_shapes=[
            pltpu.VMEM((n_x, n_y, rows, wide), bf16),
            pltpu.VMEM((n_x - 1, n_y, rows, wide), bf16),
            pltpu.VMEM((n_x - 1, n_y, rows, wide), bf16),
            pltpu.VMEM((n_y, rows, wide), f32),
            pltpu.VMEM((n_y - 1, rows, wide), bf16),
            pltpu.VMEM((n_y - 1, rows, wide), bf16),
            pltpu.VMEM((n_l, 16, wide), bf16),
            pltpu.VMEM((n_l - 1, 16, wide), bf16),
            pltpu.VMEM((2, 16, wide), f32),
            pltpu.VMEM((2, 16, wide), f32),
            pltpu.SemaphoreType.DMA((2, n_x)),
            pltpu.SemaphoreType.DMA((2, n_x - 1)),
            pltpu.SemaphoreType.DMA((2, n_y - 1)),
            pltpu.SemaphoreType.DMA((2, n_l - 1)),
            pltpu.SemaphoreType.DMA((2, 2)),
        ],
        compiler_params=pltpu.CompilerParams(
            collective_id=0, has_side_effects=True, vmem_limit_bytes=24 << 20
        ),
        name="reduce",
    )(g)


def on_device(
    tokens,
    norm_gain,
    w_qkv,
    w_out,
    obs_vectors,
    obs_lat,
    obs_cell,
    obs_count,
    shift_offsets,
    cotangent,
):
    n_batch, levels, lat_dev, lon_dev, d_model = tokens.shape
    n_lat = lax.axis_size("lat")
    n_dp = lax.axis_size("dp")
    n_hi = 4
    n_x = lax.axis_size("lon") // n_hi
    obs_rows = obs_vectors.shape[0]
    capacity = obs_rows * 3 // (2 * n_lat)
    n_slots = n_lat * capacity
    destination = obs_lat[:, 0]
    one_hot = (destination[:, None] == jnp.arange(n_lat, dtype=jnp.int32)[None, :]).astype(
        jnp.int32
    )
    earlier = jnp.cumsum(one_hot, axis=0) - one_hot
    rank_in = jnp.sum(earlier * one_hot, axis=1)
    slot_of = destination * capacity + rank_in
    is_live = jnp.arange(obs_rows, dtype=jnp.int32) < obs_count[0]
    cell_tag = jnp.where(is_live, obs_cell, -1)
    chooser = slot_of[None, :] == jnp.arange(n_slots, dtype=jnp.int32)[:, None]
    sent_rows = (
        jnp.dot(chooser.astype(jnp.bfloat16), obs_vectors, preferred_element_type=jnp.float32)
        .astype(jnp.bfloat16)
        .reshape(n_lat, capacity, d_model)
    )
    sent_tags = (jnp.sum(chooser.astype(jnp.int32) * (cell_tag[None, :] + 1), axis=1) - 1).reshape(
        n_lat, capacity
    )
    got_rows, got_tags = (
        lax.all_to_all(sent_rows, "lat", split_axis=0, concat_axis=0, tiled=True),
        lax.all_to_all(sent_tags, "lat", split_axis=0, concat_axis=0, tiled=True),
    )
    flat_tokens = tokens.reshape(-1, d_model)
    placer = (
        got_tags.reshape(-1)[None, :] == jnp.arange(flat_tokens.shape[0], dtype=jnp.int32)[:, None]
    ).astype(jnp.bfloat16)
    added = jnp.dot(placer, got_rows.reshape(-1, d_model), preferred_element_type=jnp.float32)
    enriched = (flat_tokens.astype(jnp.float32) + added).astype(jnp.bfloat16).reshape(tokens.shape)
    margin = WIN - 1
    east_cols = shifted(enriched[:, :, :, :margin], "lon", -1)
    widened = jnp.concatenate([enriched, east_cols], axis=3)
    north_part = from_behind(widened[:, :, :margin], "lat", -1)
    extended = jnp.concatenate([widened, north_part], axis=2)
    lat_shift = shift_offsets[0, 0]
    lon_shift = shift_offsets[0, 1]
    anchor = jnp.zeros((), jnp.int32)
    region = lax.dynamic_slice(
        extended, (anchor, anchor, lat_shift, lon_shift, anchor), tokens.shape
    )[0]
    base = jnp.stack([lax.axis_index("lat") * lat_dev + lat_shift, jnp.int32(lat_dev * n_lat)])
    n_tok = levels * lat_dev * lon_dev
    mixed, partial_sums = run_block(
        base,
        region.reshape(n_tok, d_model),
        norm_gain[None, :],
        w_qkv,
        w_out,
        cotangent.reshape(n_tok, d_model),
        (2, n_x, n_dp, d_model // (2 * n_dp), d_model // n_x),
    )
    reduced = run_reduce(partial_sums, n_hi)
    wide = d_model // (n_x * n_hi)
    start = (lax.axis_index("lon") % n_hi) * wide
    gradient = lax.dynamic_slice(reduced, (anchor, start), (reduced.shape[0], wide)).T
    return (mixed.reshape(tokens.shape), gradient)


def solution(mesh):
    placed = (
        P("dp", None, "lat", "lon", None),
        P(),
        P(),
        P(),
        P(("lon", "lat", "dp"), None),
        P(("lon", "lat", "dp"), None),
        P(("lon", "lat", "dp")),
        P(("lon", "lat", "dp")),
        P("dp", None),
        P("dp", None, "lat", "lon", None),
    )
    return jax.shard_map(
        on_device,
        mesh=mesh,
        in_specs=placed,
        out_specs=(P("dp", None, "lat", "lon", None), P("lon", ("lat", "dp"))),
        check_vma=False,
    )
```

time: 887 us -> 182 us (0.21); the launches traced: 872 us -> 180 us
  waiting for transfers between devices: 758 us -> 61.6 us
  Pallas kernels: 0 us -> 60.3 us
  local copies, waits for them, and re-layouts: 33.8 us -> 8.61 us
  matrix products: 17.3 us -> 0.6 us
  between operations: 19.6 us -> 6.1 us
    reduce_scatter x1 -> x0, waiting for transfers between devices: 428 us -> none  [on_device(): lax.psum_scatter(partial_rows, ('lat', 'dp'), scatter_dimension=1, tiled=...]
    unnamed x3 -> x0, waiting for transfers between devices: 271 us -> none
    pallas_call x0 -> x2, Pallas kernels: none -> 60.3 us  [the longest x1 54.9 us: run_reduce(): pl.pallas_call(functools.partial(reduce_kernel, n_x, n_y, n_h, n_l), out_...]
    unnamed x19 -> x16, local copies, waits for them, and re-layouts: 17.2 us -> 3.62 us
    dot_general x4 -> x0, matrix products: 12.4 us -> none  [the longest x1 5.73 us: window_block(): jnp.dot(normed.reshape(-1, d_model), w_qkv, preferred_element_type=jnp.fl...]
  transfers between devices with their start and end apart: 6 -> 4, of which waited for: 6 -> 4; matrix products, arithmetic and copies ran while one was open for 1% -> 2% of each run, Pallas kernels for 0% -> 0%
where the time goes in v1:
time: 182 us; the launch traced here: 180 us
  waiting for transfers between devices  61.6 us (34%)
  Pallas kernels  60.3 us (33%)
  starting transfers between devices  37.4 us (21%)
  local copies, waits for them, and re-layouts  8.61 us (5%)
  between operations  6.1 us (3%)
  other arithmetic  5.44 us (3%)
    pallas_call x1, Pallas kernels, run_reduce(): pl.pallas_call(functools.partial(reduce_kernel, n_x, n_y, n_h, n_l), out_...  54.9 us
    ppermute x1, waiting for transfers between devices, shifted(): lax.ppermute(array, axis, [(i, (i + by) % devices) for i in range(devices)])  29.6 us
    all_to_all x1, starting transfers between devices, on_device(): lax.all_to_all(sent_tags, 'lat', split_axis=0, concat_axis=0, tiled=True)  17.4 us
    all_to_all x1, waiting for transfers between devices, on_device(): lax.all_to_all(sent_rows, 'lat', split_axis=0, concat_axis=0, tiled=True)  15.8 us
    ppermute x1, starting transfers between devices, shifted(): lax.ppermute(array, axis, [(i, (i + by) % devices) for i in range(devices)])  14 us
    all_to_all x1, waiting for transfers between devices, on_device(): lax.all_to_all(sent_tags, 'lat', split_axis=0, concat_axis=0, tiled=True)  8.63 us
    ppermute x1, waiting for transfers between devices, from_behind(): return lax.ppermute(array, axis, pairs)  7.64 us
    pallas_call x1, Pallas kernels, run_block(): pl.pallas_call(block_kernel, out_shape=(jax.ShapeDtypeStruct((n_tok, d_mo...  5.35 us
  transfers between devices with their start and end apart: 4, of which 4 were waited for; matrix products, arithmetic and copies ran while one was open for 2% of the time, Pallas kernels for 0%

profile of v1, /device:TPU:1, one launch (start us, length us, event | category | flops | bytes accessed | tf_op | source)
XLA Modules:
  0.0 180.0 jit_solution(82453268741313228)
XLA Ops:
  0.6 0.0 copy-start
  0.6 0.0 copy-start.5
  1.4 0.7 fusion.3
  2.1 0.1 reduce_window_sum.11
  2.2 0.8 select_reduce_fusion.1
  3.0 0.7 fusion.5
  3.7 0.1 select_reduce_fusion
  3.8 0.7 sub.11
  4.5 17.4 %all-to-all-start = ((s32[16,1,6]{2,1,0:T(1,128)}), s32[16,1,6]{2,1,0:T(1,128)S(1)}, u32[]{:S(2)}, u32[]{:S(2)}) async-start(s32[16,1,6]{2,1,0:T(1,128)} %bitcast.5), calls=%async_computation | async-start | bytes 16384 | tf_op jit(solution)/shard_map/all_to_all | solution.py:286
  21.9 0.0 copy-done
  21.9 0.3 convolution_convert_fusion
  22.2 0.8 reshape.50
  23.0 8.6 %all-to-all-done = s32[16,1,6]{2,1,0:T(1,128)S(1)} async-done(((s32[16,1,6]{2,1,0:T(1,128)}), s32[16,1,6]{2,1,0:T(1,128)S(1)}, u32[]{:S(2)}, u32[]{:S(2)}) %all-to-all-start) | async-done | bytes 416 | tf_op jit(solution)/shard_map/all_to_all | solution.py:286
  31.6 4.0 %all-to-all-start.1 = ((bf16[16,6,1024]{2,1,0:T(8,128)(2,1)}), bf16[16,6,1024]{2,1,0:T(8,128)(2,1)S(1)}, u32[]{:S(2)}, u32[]{:S(2)}) async-start(bf16[16,6,1024]{2,1,0:T(8,128)(2,1)} %reshape.50), calls=%async_computation.1 | async-start | bytes 524288 | tf_op jit(solution)/shard_map/all_to_all | solution.py:285
  35.7 0.5 broadcast.35
  36.2 0.7 reduce.4
  36.9 0.1 eq.49
  36.9 15.8 %all-to-all-done.1 = bf16[16,6,1024]{2,1,0:T(8,128)(2,1)S(1)} async-done(((bf16[16,6,1024]{2,1,0:T(8,128)(2,1)}), bf16[16,6,1024]{2,1,0:T(8,128)(2,1)S(1)}, u32[]{:S(2)}, u32[]{:S(2)}) %all-to-all-start.1) | async-done | bytes 196640 | tf_op jit(solution)/shard_map/all_to_all | solution.py:285
  52.7 0.1 reshape.51
  52.8 0.0 copy-done.5
  52.8 0.3 fusion
  53.1 0.0 copy-start.6
  53.2 0.3 copy.21
  53.4 14.0 %collective-permute-start = (bf16[1,2,8,7,1024]{4,1,3,2,0:T(2,128)(2,1)S(1)}, bf16[1,2,8,7,1024]{4,1,3,2,0:T(2,128)(2,1)S(1)}, u32[]{:S(2)}, u32[]{:S(2)}) collective-permute-start(bf16[1,2,8,7,1024]{4,1,3,2,0:T(2,128)(2,1)S(1)} %copy.21), channel_id=1, source_target_pairs={{0,960},{64,0},{128,64},{192,128},{256,192},{320,256},{384,320},{4... | collective-permute-start | bytes 688136 | tf_op jit(solution)/shard_map/ppermute | solution.py:17
  67.4 0.5 constant_dynamic-update-slice_fusion.1
  68.0 29.6 %collective-permute-done = bf16[1,2,8,7,1024]{4,1,3,2,0:T(2,128)(2,1)S(1)} collective-permute-done((bf16[1,2,8,7,1024]{4,1,3,2,0:T(2,128)(2,1)S(1)}, bf16[1,2,8,7,1024]{4,1,3,2,0:T(2,128)(2,1)S(1)}, u32[]{:S(2)}, u32[]{:S(2)}) %collective-permute-start) | collective-permute-done | bytes 229408 | tf_op jit(solution)/shard_map/ppermute | solution.py:17
  97.5 0.2 constant_dynamic-update-slice_fusion
  97.7 0.0 copy-start.2
  97.7 0.0 copy-start.3
  97.7 0.0 copy-start.4
  97.7 1.3 slice.17
  99.0 2.0 %collective-permute-start.1 = (bf16[1,2,7,23,1024]{4,1,3,2,0:T(2,128)(2,1)}, bf16[1,2,7,23,1024]{4,1,3,2,0:T(2,128)(2,1)}, u32[]{:S(2)}, u32[]{:S(2)}) collective-permute-start(bf16[1,2,7,23,1024]{4,1,3,2,0:T(2,128)(2,1)} %slice.17), channel_id=1, source_target_pairs={{4,0},{8,4},{12,8},{16,12},{20,16},{24,20},{28,24},{32,28},{36,32}... | collective-permute-start | bytes 1978376 | tf_op jit(solution)/shard_map/ppermute | solution.py:23
  101.0 0.0 copy-done.6
  101.0 0.6 fusion.6
  106.2 0.1 pad_add_fusion.base_ref
  106.2 7.6 %collective-permute-done.1 = bf16[1,2,7,23,1024]{4,1,3,2,0:T(2,128)(2,1)} collective-permute-done((bf16[1,2,7,23,1024]{4,1,3,2,0:T(2,128)(2,1)}, bf16[1,2,7,23,1024]{4,1,3,2,0:T(2,128)(2,1)}, u32[]{:S(2)}, u32[]{:S(2)}) %collective-permute-start.1) | collective-permute-done | bytes 659488 | tf_op jit(solution)/shard_map/ppermute | solution.py:23
  113.9 2.2 %fusion.1 = bf16[1,2,8,16,1024]{4,1,3,2,0:T(2,128)(2,1)S(1)} fusion(s32[]{:T(128)S(6)} %select_n.21, s32[]{:T(128)S(6)} %select_n.22, bf16[1,2,8,23,1024]{4,1,3,2,0:T(2,128)(2,1)S(1)} %constant_dynamic-update-slice_fusion, bf16[1,2,7,23,1024]{4,1,3,2,0:T(2,128)(2,1)} %collective-permute-done.1), kind=kLoop, calls=%fused_computation.5 | loop fusion | flops 262144 | bytes 1937416 | tf_op jit(solution)/shard_map/concatenate | solution.py:298
  116.1 0.1 copy.19
  116.2 0.0 copy-done.2
  116.2 0.0 copy-done.3
  116.3 0.0 copy-done.4
  116.3 0.0 copy-start.1
  116.3 2.8 %copy-done.1 = bf16[1024,3072]{1,0:T(8,128)(2,1)S(1)} copy-done((bf16[1024,3072]{1,0:T(8,128)(2,1)S(1)}, bf16[1024,3072]{1,0:T(8,128)(2,1)}, u32[]{:S(2)}) %copy-start.1) | copy-done | bytes 6291480
  119.1 5.3 %block.1 = (bf16[256,1024]{1,0:T(8,128)(2,1)}, bf16[2,4,4,128,256]{4,3,2,1,0:T(8,128)(2,1)S(1)}) custom-call(s32[2]{0:T(128)S(1)} %pad_add_fusion.base_ref, bf16[256,1024]{1,0:T(8,128)(2,1)S(1)} %bitcast.19, f32[1,1024]{1,0:T(1,128)S(1)} %bitcast.21, bf16[1024,3072]{1,0:T(8,128)(2,1)S(1)} %copy-done.1, bf16[1024,1024]{1,0:T(8,128)(2,1)S(1)} %copy-done.2, ...), custom_call_target="tpu_custom_call" | custom-call | flops 3221225472 | bytes 12582912 | tf_op jit(solution)/shard_map/block/pallas_call | solution.py:92
  124.4 54.9 %reduce.5 = f32[16,256]{1,0:T(8,128)S(1)} custom-call(bf16[2,4,4,128,256]{4,3,2,1,0:T(8,128)(2,1)S(1)} %get-tuple-element.5.g_ref), custom_call_target="tpu_custom_call" | custom-call | tf_op jit(solution)/shard_map/reduce/pallas_call | solution.py:217
  179.3 0.7 dynamic-slice_bitcast_fusion
  (2 shorter events, 0.0 us)
Async XLA Ops:
  0.6 21.3 %copy-start = (bf16[64,1024]{1,0:T(8,128)(2,1)S(1)}, bf16[64,1024]{1,0:T(8,128)(2,1)}, u32[]{:S(2)}) copy-start(bf16[64,1024]{1,0:T(8,128)(2,1)} %param.14) | copy-start | bytes 393220
  0.6 52.2 %copy-start.5 = (bf16[1,2,8,16,1024]{4,3,2,1,0:T(8,128)(2,1)S(1)}, bf16[1,2,8,16,1024]{4,3,2,1,0:T(8,128)(2,1)}, u32[]{:S(2)}) copy-start(bf16[1,2,8,16,1024]{4,3,2,1,0:T(8,128)(2,1)} %param.10) | copy-start | bytes 1572868
  4.5 27.1 %all-to-all-start = ((s32[16,1,6]{2,1,0:T(1,128)}), s32[16,1,6]{2,1,0:T(1,128)S(1)}, u32[]{:S(2)}, u32[]{:S(2)}) async-start(s32[16,1,6]{2,1,0:T(1,128)} %bitcast.5), calls=%async_computation | async-start | bytes 16384 | tf_op jit(solution)/shard_map/all_to_all | solution.py:286
  31.6 21.1 %all-to-all-start.1 = ((bf16[16,6,1024]{2,1,0:T(8,128)(2,1)}), bf16[16,6,1024]{2,1,0:T(8,128)(2,1)S(1)}, u32[]{:S(2)}, u32[]{:S(2)}) async-start(bf16[16,6,1024]{2,1,0:T(8,128)(2,1)} %reshape.50), calls=%async_computation.1 | async-start | bytes 524288 | tf_op jit(solution)/shard_map/all_to_all | solution.py:285
  53.1 47.9 %copy-start.6 = (s32[1,2]{1,0:T(1,128)S(1)}, s32[1,2]{1,0:T(1,128)}, u32[]{:S(2)}) copy-start(s32[1,2]{1,0:T(1,128)} %param.18) | copy-start | bytes 28
  53.4 44.1 %collective-permute-start = (bf16[1,2,8,7,1024]{4,1,3,2,0:T(2,128)(2,1)S(1)}, bf16[1,2,8,7,1024]{4,1,3,2,0:T(2,128)(2,1)S(1)}, u32[]{:S(2)}, u32[]{:S(2)}) collective-permute-start(bf16[1,2,8,7,1024]{4,1,3,2,0:T(2,128)(2,1)S(1)} %copy.21), channel_id=1, source_target_pairs={{0,960},{64,0},{128,64},{192,128},{256,192},{320,256},{384,320},{4... | collective-permute-start | bytes 688136 | tf_op jit(solution)/shard_map/ppermute | solution.py:17
  97.7 18.5 %copy-start.2 = (bf16[1024,1024]{1,0:T(8,128)(2,1)S(1)}, bf16[1024,1024]{1,0:T(8,128)(2,1)}, u32[]{:S(2)}) copy-start(bf16[1024,1024]{1,0:T(8,128)(2,1)} %w_out_ref.1) | copy-start | bytes 6291460
  97.7 18.5 %copy-start.3 = (bf16[1,2,8,16,1024]{4,3,2,1,0:T(8,128)(2,1)S(1)}, bf16[1,2,8,16,1024]{4,3,2,1,0:T(8,128)(2,1)}, u32[]{:S(2)}) copy-start(bf16[1,2,8,16,1024]{4,3,2,1,0:T(8,128)(2,1)} %param.19) | copy-start | bytes 1572868
  97.7 18.5 %copy-start.4 = (f32[1024]{0:T(1024)S(1)}, f32[1024]{0:T(1024)}, u32[]{:S(2)}) copy-start(f32[1024]{0:T(1024)} %param.11) | copy-start | bytes 12292
  99.0 14.8 %collective-permute-start.1 = (bf16[1,2,7,23,1024]{4,1,3,2,0:T(2,128)(2,1)}, bf16[1,2,7,23,1024]{4,1,3,2,0:T(2,128)(2,1)}, u32[]{:S(2)}, u32[]{:S(2)}) collective-permute-start(bf16[1,2,7,23,1024]{4,1,3,2,0:T(2,128)(2,1)} %slice.17), channel_id=1, source_target_pairs={{4,0},{8,4},{12,8},{16,12},{20,16},{24,20},{28,24},{32,28},{36,32}... | collective-permute-start | bytes 1978376 | tf_op jit(solution)/shard_map/ppermute | solution.py:23
  116.3 2.8 %copy-start.1 = (bf16[1024,3072]{1,0:T(8,128)(2,1)S(1)}, bf16[1024,3072]{1,0:T(8,128)(2,1)}, u32[]{:S(2)}) copy-start(bf16[1024,3072]{1,0:T(8,128)(2,1)} %w_qkv_ref.1) | copy-start | bytes 18874372

commit v2 on v1

v2 whole, which is shorter than its diff:
```python
import functools

import jax
import jax.numpy as jnp
from jax import lax
from jax.experimental import pallas as pl
from jax.experimental.pallas import tpu as pltpu
from jax.sharding import PartitionSpec as P

HEADS = 16
WIN = 8
MESH = pl.DeviceIdType.MESH


def exchange_kernel(
    n_x, n_h,
    count_ref, tok_hbm, obs_hbm, lat_hbm, cell_hbm, gain_hbm, w_qkv_hbm, w_out_hbm, cot_hbm,
    own_ref, next_ref, gain_ref, w_qkv_ref, w_out_ref, cot_ref,
    tok_ref, obs_ref, lat_ref, cell_ref, send, recv, l_sems, o_sems, e_sems, n_sems, c_sems,
):
    loads = []
    for src, dst in (
        (lat_hbm, lat_ref), (cell_hbm, cell_ref), (obs_hbm, obs_ref), (tok_hbm, tok_ref),
        (gain_hbm, gain_ref), (cot_hbm, cot_ref), (w_qkv_hbm, w_qkv_ref), (w_out_hbm, w_out_ref),
    ):
        loads.append(pltpu.make_async_copy(src, dst, l_sems.at[len(loads)]))
        loads[-1].start()
    lon, lat = lax.axis_index("lon"), lax.axis_index("lat")
    n_lon = n_x * n_h
    n_lat = send.shape[0]
    f32, bf16, i32 = jnp.float32, jnp.bfloat16, jnp.int32
    west = {"lon": (lon + n_lon - 1) % n_lon}
    east = {"lon": (lon + 1) % n_lon}
    south = {"lat": (lat + n_lat - 1) % n_lat}
    others = [{"lat": (lat + k) % n_lat} for k in range(1, n_lat)]
    barrier = pltpu.get_barrier_semaphore()
    for peer in others + [west, east]:
        pl.semaphore_signal(barrier, inc=1, device_id=peer, device_id_type=MESH)

    for one in loads[:3]:
        one.wait()
    n_obs, d_model = obs_ref.shape
    n_slots = n_lat * 8
    slot = lax.broadcasted_iota(i32, (n_slots, n_obs), 0)
    bound = lat_ref[...] == slot // 8
    earlier = lax.broadcasted_iota(i32, (n_obs, n_obs), 0) < lax.broadcasted_iota(i32, (n_obs, n_obs), 1)
    rank = jnp.dot(bound.astype(f32).astype(bf16), earlier.astype(f32).astype(bf16), preferred_element_type=f32)
    chooser = jnp.where(bound & (rank == (slot % 8).astype(f32)), 1.0, 0.0).astype(bf16)
    rows = jnp.dot(chooser, obs_ref[...], preferred_element_type=f32).reshape(n_lat, 8, d_model)
    live = lax.broadcasted_iota(i32, (8, n_obs), 1) < count_ref[0]
    tags = jnp.where(live, cell_ref[...] + 1, 0).astype(f32).astype(bf16)
    tags = lax.dot_general(tags, chooser, (((1,), (1,)), ((), ())), preferred_element_type=f32)
    at_tag = lax.broadcasted_iota(i32, (n_lat, 8, n_slots), 1) == 6
    send[:, :, :n_slots] = jnp.where(at_tag, tags[None], rows[:, :, :n_slots]).astype(bf16)
    send[:, :, n_slots:] = rows[:, :, n_slots:].astype(bf16)
    recv[lat] = send[lat]

    pl.semaphore_wait(barrier, len(others) + 2)

    def copy(src, dst, sems, k, where):
        return pltpu.make_async_remote_copy(
            src_ref=src, dst_ref=dst, send_sem=sems.at[0, k], recv_sem=sems.at[1, k],
            device_id=where, device_id_type=MESH,
        )

    o_copies = [
        copy(send.at[(lat + k) % n_lat], recv.at[lat], o_sems, k - 1, others[k - 1]) for k in range(1, n_lat)
    ]
    for one in o_copies:
        one.start()
    loads[3].wait()
    n_col, col_rows, _ = own_ref.shape
    lon_dev = tok_ref.shape[0] // col_rows
    margin = n_col - lon_dev
    n_tok = lon_dev * col_rows
    place = lax.broadcasted_iota(i32, (n_tok, n_tok), 0)
    cell = (place % col_rows) * lon_dev + place // col_rows
    mover = jnp.where(cell == lax.broadcasted_iota(i32, (n_tok, n_tok), 1), 1.0, 0.0).astype(bf16)
    turned = jnp.dot(mover, tok_ref[...], preferred_element_type=f32)
    for one in o_copies:
        one.wait_recv()
    got = recv[...].astype(f32)
    slots = got[:, :, :n_slots]
    sub = lax.broadcasted_iota(i32, slots.shape, 1)
    tag = jnp.sum(jnp.where(sub == 6, slots, 0.0), axis=1, keepdims=True)
    lane = lax.broadcasted_iota(i32, slots.shape, 2)
    tag = jnp.sum(jnp.where(lane == lat * 8 + sub, tag, 0.0), axis=2, keepdims=True)
    tag = tag.reshape(n_slots, 1)
    place = lax.broadcasted_iota(i32, (n_slots, n_tok), 1)
    cell = (place % col_rows) * lon_dev + place // col_rows + 1
    placer = jnp.where(tag == cell.astype(f32), 1.0, 0.0).astype(bf16)
    added = lax.dot_general(
        placer, got.reshape(n_slots, d_model).astype(bf16), (((0,), (0,)), ((), ())), preferred_element_type=f32
    )
    own_ref[:lon_dev] = (turned + added).astype(bf16).reshape(lon_dev, col_rows, d_model)

    e_copies = [copy(own_ref.at[j], own_ref.at[lon_dev + j], e_sems, j, west) for j in range(margin)]
    for one in e_copies:
        one.start()
    half = lon_dev // 2
    n_copies = [
        copy(own_ref.at[pl.ds(h * half, half)], next_ref.at[pl.ds(h * half, half)], n_sems, h, south)
        for h in range(2)
    ]
    c_copies = [
        copy(own_ref.at[lon_dev + j], next_ref.at[lon_dev + j], c_sems, j, south) for j in range(margin)
    ]

    @pl.when(lat > 0)
    def _():
        for one in n_copies:
            one.start()

    @pl.when(lat == n_lat - 1)
    def _():
        next_ref[...] = jnp.zeros_like(next_ref)

    for j in range(margin):
        e_copies[j].wait_recv()

        @pl.when(lat > 0)
        def _():
            c_copies[j].start()

    @pl.when(lat < n_lat - 1)
    def _():
        for one in n_copies + c_copies:
            one.wait_recv()

    @pl.when(lat > 0)
    def _():
        for one in n_copies + c_copies:
            one.wait_send()

    for one in o_copies + e_copies:
        one.wait_send()
    for one in loads[4:]:
        one.wait()


def run_exchange(count, arrays, n_lat, n_x, n_h, n_col, col_rows):
    tokens, obs, lats, cells = arrays[:4]
    d_model = obs.shape[1]
    margin = WIN - 1
    vmem = pl.BlockSpec(memory_space=pltpu.VMEM)
    bf16 = jnp.bfloat16
    block = jax.ShapeDtypeStruct((n_col, col_rows, d_model), bf16)
    return pl.pallas_call(
        functools.partial(exchange_kernel, n_x, n_h),
        out_shape=[block, block] + [jax.ShapeDtypeStruct(one.shape, one.dtype) for one in arrays[4:]],
        in_specs=[pl.BlockSpec(memory_space=pltpu.SMEM)] + [pl.BlockSpec(memory_space=pltpu.HBM)] * len(arrays),
        out_specs=[vmem] * (len(arrays) - 2),
        scratch_shapes=[
            pltpu.VMEM(tokens.shape, bf16),
            pltpu.VMEM(obs.shape, bf16),
            pltpu.VMEM(lats.shape, jnp.int32),
            pltpu.VMEM(cells.shape, jnp.int32),
            pltpu.VMEM((n_lat, 8, d_model), bf16),
            pltpu.VMEM((n_lat, 8, d_model), bf16),
            pltpu.SemaphoreType.DMA((len(arrays),)),
            pltpu.SemaphoreType.DMA((2, n_lat - 1)),
            pltpu.SemaphoreType.DMA((2, margin)),
            pltpu.SemaphoreType.DMA((2, 2)),
            pltpu.SemaphoreType.DMA((2, margin)),
        ],
        compiler_params=pltpu.CompilerParams(
            collective_id=1, has_side_effects=True, vmem_limit_bytes=32 << 20
        ),
        cost_estimate=pl.CostEstimate(flops=1 << 28, bytes_accessed=80 << 20, transcendentals=0),
        name="exchange",
    )(count, *[pltpu.with_memory_space_constraint(one, pltpu.HBM) for one in arrays])


def block_kernel(
    lat_dev, shift_ref, own_ref, next_ref, gain_ref, w_qkv_ref, w_out_ref, cot_ref, out_ref, g_ref,
    region_ref, qkv_ref, ctx_ref, ctx_t_ref,
):
    n_tok, d_model = region_ref.shape
    n_src = own_ref.shape[0]
    lon_dev = 2 * WIN
    col_rows = n_tok // lon_dev
    lat_shift, lon_shift = shift_ref[0, 0], shift_ref[0, 1]
    base = lax.axis_index("lat") * lat_dev + lat_shift
    limit = lax.axis_size("lat") * lat_dev
    token = lax.broadcasted_iota(jnp.int32, (n_tok, n_src), 0)
    row = (token // lon_dev) % lat_dev + lat_shift
    source = (token % lon_dev + lon_shift) * col_rows + (token // (lon_dev * lat_dev)) * lat_dev + row
    source = source - lax.broadcasted_iota(jnp.int32, (n_tok, n_src), 1)
    here = jnp.where((source == 0) & (row < lat_dev), 1.0, 0.0).astype(jnp.bfloat16)
    after = jnp.where((source == lat_dev) & (row >= lat_dev), 1.0, 0.0)
    after = jnp.where(row + lax.axis_index("lat") * lat_dev < limit, after, 0.0).astype(jnp.bfloat16)
    region_ref[...] = jnp.dot(here, own_ref[...], preferred_element_type=jnp.float32) + jnp.dot(
        after, next_ref[...], preferred_element_type=jnp.float32
    )
    head_dim = d_model // HEADS
    pair = 2 * head_dim
    groups = n_tok // (2 * WIN)
    win_tok = n_tok // 2
    as_float = region_ref[...]
    average = jnp.mean(as_float, axis=-1, keepdims=True)
    centred = as_float - average
    variance = jnp.mean(centred * centred, axis=-1, keepdims=True)
    normed = (centred * lax.rsqrt(variance + 1e-05) * gain_ref[...]).astype(jnp.bfloat16)
    block = 512
    for col in range(0, 3 * d_model, block):
        part = jnp.dot(normed, w_qkv_ref[:, col : col + block], preferred_element_type=jnp.float32)
        part = part.reshape(groups, 2, WIN, block)
        for win in range(2):
            qkv_ref[win, :, col : col + block] = part[:, win].reshape(win_tok, block).astype(jnp.bfloat16)
    lane = lax.broadcasted_iota(jnp.int32, (win_tok, pair), 1)
    first = lane < head_dim
    key = lax.broadcasted_iota(jnp.int32, (win_tok, 2 * win_tok), 1)
    is_valid = base + (key // WIN) % WIN < limit
    for win in range(2):
        for two in range(HEADS // 2):
            at = two * pair
            queries = qkv_ref[win, :, at : at + pair]
            keys = qkv_ref[win, :, d_model + at : d_model + at + pair]
            values = qkv_ref[win, :, 2 * d_model + at : 2 * d_model + at + pair]
            zero = jnp.zeros_like(keys)
            keys = jnp.concatenate([jnp.where(first, keys, zero), jnp.where(first, zero, keys)], axis=0)
            values = jnp.concatenate([jnp.where(first, values, zero), jnp.where(first, zero, values)], axis=0)
            scores = lax.dot_general(
                queries, keys, (((1,), (1,)), ((), ())), preferred_element_type=jnp.float32
            ) * head_dim ** (-0.5)
            scores = jnp.where(is_valid, scores, -1e30)
            weights = []
            for half in range(2):
                mine = scores[:, half * win_tok : (half + 1) * win_tok]
                powers = jnp.exp(mine - jnp.max(mine, axis=-1, keepdims=True))
                weights.append((powers / jnp.sum(powers, axis=-1, keepdims=True)).astype(jnp.bfloat16))
            context = jnp.dot(jnp.concatenate(weights, axis=1), values, preferred_element_type=jnp.float32)
            ctx_ref[:, win, :, at : at + pair] = context.reshape(groups, WIN, pair)
    context = ctx_ref[...].reshape(n_tok, d_model).astype(jnp.bfloat16)
    for col in range(0, d_model, block):
        result = jnp.dot(context, w_out_ref[:, col : col + block], preferred_element_type=jnp.float32)
        out_ref[:, col : col + block] = (region_ref[:, col : col + block] + result).astype(jnp.bfloat16)
    ctx_t_ref[...] = context.T
    cores, n_x, n_y, rows, wide = g_ref.shape
    n_z = rows // 16
    for x in range(n_x):
        part = jnp.dot(
            ctx_t_ref[...], cot_ref[:, x * wide : (x + 1) * wide], preferred_element_type=jnp.float32
        ).astype(jnp.bfloat16)
        for z in range(n_z):
            for core in range(cores):
                for y in range(n_y):
                    at = ((z * cores + core) * n_y + y) * 16
                    g_ref[core, x, y, z * 16 : (z + 1) * 16, :] = part[at : at + 16, :]


def run_block(lat_dev, shift, own, after, gain, w_qkv, w_out, cot, dims):
    n_tok, d_model = cot.shape
    vmem = pl.BlockSpec(memory_space=pltpu.VMEM)
    return pl.pallas_call(
        functools.partial(block_kernel, lat_dev),
        out_shape=(
            jax.ShapeDtypeStruct((n_tok, d_model), jnp.bfloat16),
            jax.ShapeDtypeStruct(dims, jnp.bfloat16),
        ),
        in_specs=[pl.BlockSpec(memory_space=pltpu.SMEM)] + [vmem] * 6,
        out_specs=(vmem, vmem),
        scratch_shapes=[
            pltpu.VMEM((n_tok, d_model), jnp.float32),
            pltpu.VMEM((2, n_tok // 2, 3 * d_model), jnp.bfloat16),
            pltpu.VMEM((n_tok // (2 * WIN), 2, WIN, d_model), jnp.float32),
            pltpu.VMEM((d_model, n_tok), jnp.bfloat16),
        ],
        compiler_params=pltpu.CompilerParams(vmem_limit_bytes=40 << 20),
        cost_estimate=pl.CostEstimate(flops=3 << 30, bytes_accessed=12 << 20, transcendentals=1 << 19),
        name="block",
    )(shift, own, after, gain, w_qkv, w_out, cot)


def reduce_kernel(
    n_x, n_y, n_h, n_l,
    g_ref, out_ref,
    c_recv_a, c_recv_b, x_send, x_recv, x_sum, y_send, y_recv, y_sum,
    a_send, a_recv, b_send, b_recv, l_send, l_recv, h_send, h_recv, t_send, t_recv,
    c_sems, x_sems, y_sems, a_sems, b_sems, l_sems, h_sems,
):
    lon, lat, y = lax.axis_index("lon"), lax.axis_index("lat"), lax.axis_index("dp")
    x, z_hi = lon // n_h, lon % n_h
    z_lo, core = lat // 2, lat % 2
    f32, bf16 = jnp.float32, jnp.bfloat16

    def at_x(k):
        return {"lon": ((x + k) % n_x) * n_h + z_hi}

    def at_y(k):
        return {"dp": (y + k) % n_y}

    def at_l(k):
        return {"lat": ((z_lo + k) % n_l) * 2 + core}

    def at_h(other):
        return {"lon": x * n_h + other}

    pal = {"lat": z_lo * 2 + 1 - core}
    near = z_hi + 1 - 2 * (z_hi % 2)
    far = (z_hi + n_h - 1 + 2 * (z_hi % 2)) % n_h
    peers = [pal] + [at_x(k) for k in range(1, n_x)] + [at_y(k) for k in range(1, n_y)]
    peers += [at_l(k) for k in range(1, n_l)] + [at_h(near), at_h(far)]
    barrier = pltpu.get_barrier_semaphore()
    for peer in peers:
        pl.semaphore_signal(barrier, inc=1, device_id=peer, device_id_type=MESH)
    pl.semaphore_wait(barrier, len(peers))
    copies = []

    def send(src, dst, sems, k, where):
        one = pltpu.make_async_remote_copy(
            src_ref=src, dst_ref=dst, send_sem=sems.at[0, k], recv_sem=sems.at[1, k],
            device_id=where, device_id_type=MESH,
        )
        one.start()
        copies.append(one)
        return one

    _, _, _, rows, wide = g_ref.shape
    half = rows // 2
    low, high = pl.ds(0, half), pl.ds(half, half)
    order = [2, 1, 3, 0]
    c_a, c_b = {}, {}
    for i, k in enumerate(order):
        dest = (x + k) % n_x
        c_a[k] = send(g_ref.at[1 - core, dest, :, low], c_recv_a.at[k], c_sems, 2 * i, pal)
        dest = (y + k) % n_y
        c_b[k] = send(g_ref.at[1 - core, :, dest, high], c_recv_b.at[k], c_sems, 2 * i + 1, pal)
    x_c, y_c = {}, {}
    for k in order:
        c_a[k].wait_recv()
        dest = (x + k) % n_x
        for i in range(n_y):
            part = g_ref[core, dest, i, :half].astype(f32) + c_recv_a[k, i].astype(f32)
            if k:
                x_send[k - 1, i] = part.astype(bf16)
            else:
                x_sum[i] = part
        if k:
            x_c[k] = send(x_send.at[k - 1], x_recv.at[k - 1], x_sems, k - 1, at_x(k))
        c_b[k].wait_recv()
        dest = (y + k) % n_y
        for i in range(n_x):
            part = g_ref[core, i, dest, half:].astype(f32) + c_recv_b[k, i].astype(f32)
            if k:
                y_send[k - 1, i] = part.astype(bf16)
            else:
                y_sum[i] = part
        if k:
            y_c[k] = send(y_send.at[k - 1], y_recv.at[k - 1], y_sems, k - 1, at_y(k))
    for k in range(1, n_x):
        x_c[k].wait_recv()
    a_c, b_c = {}, {}
    for k in order:
        dest = (y + k) % n_y
        part_a = x_sum[dest]
        for j in range(n_x - 1):
            part_a = part_a + x_recv[j, dest].astype(f32)
        if k:
            a_send[k - 1] = part_a.astype(bf16)
            a_c[k] = send(a_send.at[k - 1], a_recv.at[k - 1], a_sems, k - 1, at_y(k))
    for k in range(1, n_y):
        y_c[k].wait_recv()
    for k in order:
        dest = (x + k) % n_x
        part_b = y_sum[dest]
        for j in range(n_y - 1):
            part_b = part_b + y_recv[j, dest].astype(f32)
        if k:
            b_send[k - 1] = part_b.astype(bf16)
            b_c[k] = send(b_send.at[k - 1], b_recv.at[k - 1], b_sems, k - 1, at_x(k))
    for k in range(1, n_y):
        a_c[k].wait_recv()
        part_a = part_a + a_recv[k - 1].astype(f32)
    for k in range(1, n_x):
        b_c[k].wait_recv()
        part_b = part_b + b_recv[k - 1].astype(f32)
    x_sum[0] = part_a
    x_sum[1] = part_b
    each = rows // n_l
    l_send[: n_l // 2] = part_a.reshape(n_l // 2, each, wide).astype(bf16)
    l_send[n_l // 2 :] = part_b.reshape(n_l // 2, each, wide).astype(bf16)
    l_c = {}
    for k in range(1, n_l):
        l_c[k] = send(l_send.at[(z_lo + k) % n_l], l_recv.at[k - 1], l_sems, k - 1, at_l(k))
    mine = pl.ds(pl.multiple_of((z_lo % (n_l // 2)) * each, each), each)
    part = x_sum[z_lo // (n_l // 2), mine, :]
    for k in range(1, n_l):
        l_c[k].wait_recv()
        part = part + l_recv[k - 1].astype(f32)
    h_send[...] = part.astype(bf16)
    first = send(h_send, h_recv, h_sems, 0, at_h(near))
    first.wait_recv()
    part = part + h_recv[...].astype(f32)
    tile = wide // 2
    left, right = part[:, :tile], part[:, tile:]
    t_send[...] = jnp.where(far // 2 == 0, left, right)
    second = send(t_send, t_recv, h_sems, 1, at_h(far))
    part = jnp.where(z_hi // 2 == 0, left, right)
    second.wait_recv()
    part = part + t_recv[...]
    out_ref[...] = jnp.where(z_hi % 2 == 0, part[:, : tile // 2], part[:, tile // 2 :])
    for one in copies:
        one.wait_send()


def run_reduce(g, n_h):
    _, n_x, n_y, rows, wide = g.shape
    n_l = rows // 16
    half = rows // 2
    vmem = pl.BlockSpec(memory_space=pltpu.VMEM)
    bf16, f32 = jnp.bfloat16, jnp.float32
    sems = pltpu.SemaphoreType.DMA
    return pl.pallas_call(
        functools.partial(reduce_kernel, n_x, n_y, n_h, n_l),
        out_shape=jax.ShapeDtypeStruct((16, wide // n_h), f32),
        in_specs=[vmem],
        out_specs=vmem,
        scratch_shapes=[
            pltpu.VMEM((n_x, n_y, half, wide), bf16),
            pltpu.VMEM((n_y, n_x, half, wide), bf16),
            pltpu.VMEM((n_x - 1, n_y, half, wide), bf16),
            pltpu.VMEM((n_x - 1, n_y, half, wide), bf16),
            pltpu.VMEM((n_y, half, wide), f32),
            pltpu.VMEM((n_y - 1, n_x, half, wide), bf16),
            pltpu.VMEM((n_y - 1, n_x, half, wide), bf16),
            pltpu.VMEM((n_x, half, wide), f32),
            pltpu.VMEM((n_y - 1, half, wide), bf16),
            pltpu.VMEM((n_y - 1, half, wide), bf16),
            pltpu.VMEM((n_x - 1, half, wide), bf16),
            pltpu.VMEM((n_x - 1, half, wide), bf16),
            pltpu.VMEM((n_l, 16, wide), bf16),
            pltpu.VMEM((n_l - 1, 16, wide), bf16),
            pltpu.VMEM((16, wide), bf16),
            pltpu.VMEM((16, wide), bf16),
            pltpu.VMEM((16, wide // 2), f32),
            pltpu.VMEM((16, wide // 2), f32),
            sems((2, 2 * n_x)),
            sems((2, n_x - 1)),
            sems((2, n_y - 1)),
            sems((2, n_y - 1)),
            sems((2, n_x - 1)),
            sems((2, n_l - 1)),
            sems((2, 2)),
        ],
        compiler_params=pltpu.CompilerParams(
            collective_id=0, has_side_effects=True, vmem_limit_bytes=24 << 20
        ),
        name="reduce",
    )(g)


def on_device(
    tokens,
    norm_gain,
    w_qkv,
    w_out,
    obs_vectors,
    obs_lat,
    obs_cell,
    obs_count,
    shift_offsets,
    cotangent,
):
    n_batch, levels, lat_dev, lon_dev, d_model = tokens.shape
    n_lat = lax.axis_size("lat")
    n_dp = lax.axis_size("dp")
    n_hi = 4
    n_x = lax.axis_size("lon") // n_hi
    n_obs = obs_vectors.shape[0]
    n_col = lon_dev + WIN - 1
    arrays = (
        tokens.reshape(-1, d_model),
        obs_vectors,
        obs_lat.reshape(1, n_obs),
        obs_cell[None, :],
        norm_gain[None, :],
        w_qkv,
        w_out,
        cotangent.reshape(-1, d_model),
    )
    own, after, gain, w_qkv, w_out, cot = run_exchange(
        obs_count, arrays, n_lat, n_x, n_hi, n_col, levels * lat_dev
    )
    mixed, partial_sums = run_block(
        lat_dev,
        shift_offsets,
        own.reshape(-1, d_model),
        after.reshape(-1, d_model),
        gain,
        w_qkv,
        w_out,
        cot,
        (2, n_x, n_dp, d_model // (2 * n_dp), d_model // n_x),
    )
    reduced = run_reduce(partial_sums, n_hi)
    gradient = reduced.T
    return (mixed.reshape(tokens.shape), gradient)


def solution(mesh):
    placed = (
        P("dp", None, "lat", "lon", None),
        P(),
        P(),
        P(),
        P(("lon", "lat", "dp"), None),
        P(("lon", "lat", "dp"), None),
        P(("lon", "lat", "dp")),
        P(("lon", "lat", "dp")),
        P("dp", None),
        P("dp", None, "lat", "lon", None),
    )
    return jax.shard_map(
        on_device,
        mesh=mesh,
        in_specs=placed,
        out_specs=(P("dp", None, "lat", "lon", None), P("lon", ("lat", "dp"))),
        check_vma=False,
    )
```

time: 182 us -> 134 us (0.74)
  Pallas kernels: 60.3 us -> 130 us
  waiting for transfers between devices: 61.6 us -> 0 us
  starting transfers between devices: 37.4 us -> 0 us
  local copies, waits for them, and re-layouts: 8.61 us -> 0.61 us
  other arithmetic: 5.44 us -> 0 us
  between operations: 6.1 us -> 1.31 us
    pallas_call x1 -> x2, Pallas kernels: 5.35 us -> 93.8 us  [the longest x1 87.8 us: run_exchange(): pl.pallas_call(functools.partial(exchange_kernel, n_x, n_h), out_shape=[b...]
    ppermute x2 -> x0, waiting for transfers between devices: 37.2 us -> none  [the longest x1 29.6 us: shifted(): lax.ppermute(array, axis, [(i, (i + by) % devices) for i in range(devices)])]
    all_to_all x2 -> x0, waiting for transfers between devices: 24.4 us -> none  [the longest x1 15.8 us: on_device(): lax.all_to_all(sent_rows, 'lat', split_axis=0, concat_axis=0, tiled=True)]
    all_to_all x2 -> x0, starting transfers between devices: 21.4 us -> none  [the longest x1 17.4 us: on_device(): lax.all_to_all(sent_tags, 'lat', split_axis=0, concat_axis=0, tiled=True)]
    pallas_call x1, Pallas kernels: 54.9 us -> 36.2 us  [run_reduce(): pl.pallas_call(functools.partial(reduce_kernel, n_x, n_y, n_h, n_l), out_...]
    ppermute x2 -> x0, starting transfers between devices: 15.9 us -> none  [the longest x1 14 us: shifted(): lax.ppermute(array, axis, [(i, (i + by) % devices) for i in range(devices)])]
    unnamed x16 -> x3, local copies, waits for them, and re-layouts: 3.62 us -> 0.61 us
    concatenate x1 -> x0, other arithmetic: 2.24 us -> none  [on_device(): extended = jnp.concatenate([widened, north_part], axis=2)]
  transfers between devices with their start and end apart: 4 -> 0, of which waited for: 4 -> 0; matrix products, arithmetic and copies ran while one was open for 2% -> 0% of each run, Pallas kernels for 0% -> 0%
where the time goes in v2:
time: 134 us; the launch traced here: 132 us
  Pallas kernels  130 us (97%)
    pallas_call x1, Pallas kernels, run_exchange(): pl.pallas_call(functools.partial(exchange_kernel, n_x, n_h), out_shape=[b...  87.8 us
    pallas_call x1, Pallas kernels, run_reduce(): pl.pallas_call(functools.partial(reduce_kernel, n_x, n_y, n_h, n_l), out_...  36.2 us
    pallas_call x1, Pallas kernels, run_block(): pl.pallas_call(functools.partial(block_kernel, lat_dev), out_shape=(jax.S...  6.01 us

profile of v2, /device:TPU:1, one launch (start us, length us, event | category | flops | bytes accessed | tf_op | source)
XLA Modules:
  0.0 132.0 jit_solution(13498141494046859887)
XLA Ops:
  1.3 0.0 copy-start
  1.3 87.8 %exchange.1 = (bf16[23,16,1024]{2,1,0:T(8,128)(2,1)S(1)}, bf16[23,16,1024]{2,1,0:T(8,128)(2,1)S(1)}, f32[1,1024]{1,0:T(1,128)S(1)}, bf16[1024,3072]{1,0:T(8,128)...) custom-call(s32[1]{0:T(128)S(6)} %copy.13.count_ref, bf16[256,1024]{1,0:T(8,128)(2,1)} %bitcast.12, ...), custom_call_target="tpu_custom_call" | custom-call | flops 268435456 | bytes 83886080 | tf_op jit(solution)/shard_map/exchange/pallas_call | solution.py:148
  89.1 0.0 copy-done
  89.1 6.0 %block.1 = (bf16[256,1024]{1,0:T(8,128)(2,1)}, bf16[2,4,4,128,256]{4,3,2,1,0:T(8,128)(2,1)S(1)}) custom-call(s32[1,2]{1,0:T(1,128)S(1)} %copy-done, bf16[368,1024]{1,0:T(8,128)(2,1)S(1)} %bitcast.10, bf16[368,1024]{1,0:T(8,128)(2,1)S(1)} %bitcast.11, f32[1,1024]{1,0:T(1,128)S(1)} %get-tuple-element.12.gain_ref, ...), custom_call_target="tpu_custom_call" | custom-call | flops 3221225472 | bytes 12582912 | tf_op jit(solution)/shard_map/block/pallas_call | solution.py:255
  95.1 36.2 %reduce.1 = f32[16,64]{1,0:T(8,128)S(1)} custom-call(bf16[2,4,4,128,256]{4,3,2,1,0:T(8,128)(2,1)S(1)} %get-tuple-element.17.g_ref), custom_call_target="tpu_custom_call" | custom-call | tf_op jit(solution)/shard_map/reduce/pallas_call | solution.py:414
  131.4 0.6 copy.14
Async XLA Ops:
  1.3 87.8 %copy-start = (s32[1,2]{1,0:T(1,128)S(1)}, s32[1,2]{1,0:T(1,128)}, u32[]{:S(2)}) copy-start(s32[1,2]{1,0:T(1,128)} %shift_ref.1) | copy-start | bytes 28

commit v3 on v2

--- a/solution.py
+++ b/solution.py
@@ -12,11 +12,12 @@
 MESH = pl.DeviceIdType.MESH
 
 
-def exchange_kernel(
-    n_x, n_h,
+def exchange_part(
+    n_x, n_h, peers,
     count_ref, tok_hbm, obs_hbm, lat_hbm, cell_hbm, gain_hbm, w_qkv_hbm, w_out_hbm, cot_hbm,
     own_ref, next_ref, gain_ref, w_qkv_ref, w_out_ref, cot_ref,
-    tok_ref, obs_ref, lat_ref, cell_ref, send, recv, l_sems, o_sems, e_sems, n_sems, c_sems,
+    tok_ref, obs_ref, lat_ref, cell_ref, send, recv, r_one, r_two,
+    l_sems, o_sems, e_sems, n_sems, c_sems, r_sems,
 ):
     loads = []
     for src, dst in (
@@ -29,12 +30,19 @@
     n_lon = n_x * n_h
     n_lat = send.shape[0]
     f32, bf16, i32 = jnp.float32, jnp.bfloat16, jnp.int32
+    x, z_hi = lon // n_h, lon % n_h
     west = {"lon": (lon + n_lon - 1) % n_lon}
     east = {"lon": (lon + 1) % n_lon}
     south = {"lat": (lat + n_lat - 1) % n_lat}
     others = [{"lat": (lat + k) % n_lat} for k in range(1, n_lat)]
+    up = {"lon": x * n_h + (z_hi + 1) % n_h}
+    turn = jnp.where(z_hi == n_h - 2, n_x - 1, 0)
+    last = {"lon": ((x + turn) % n_x) * n_h + (z_hi + 1) % n_h}
+    turn = jnp.where(z_hi == n_h - 1, 1, 0)
+    before = {"lon": ((x + turn) % n_x) * n_h + (z_hi + n_h - 1) % n_h}
     barrier = pltpu.get_barrier_semaphore()
-    for peer in others + [west, east]:
+    peers = others + [west, east, last, before] + peers
+    for peer in peers:
         pl.semaphore_signal(barrier, inc=1, device_id=peer, device_id_type=MESH)
 
     for one in loads[:3]:
@@ -55,7 +63,7 @@
     send[:, :, n_slots:] = rows[:, :, n_slots:].astype(bf16)
     recv[lat] = send[lat]
 
-    pl.semaphore_wait(barrier, len(others) + 2)
+    pl.semaphore_wait(barrier, len(peers))
 
     def copy(src, dst, sems, k, where):
         return pltpu.make_async_remote_copy(
@@ -94,8 +102,22 @@
     )
     own_ref[:lon_dev] = (turned + added).astype(bf16).reshape(lon_dev, col_rows, d_model)
 
-    e_copies = [copy(own_ref.at[j], own_ref.at[lon_dev + j], e_sems, j, west) for j in range(margin)]
-    for one in e_copies:
+    wide = d_model // 2
+    direct = [(j, 0, d_model) for j in range(margin - 2)] + [(margin - 2, 0, wide)]
+    around = [(margin - 2, wide, wide), (margin - 1, 0, wide), (margin - 1, wide, wide)]
+
+    def part_of(ref, col, piece):
+        return ref.at[col + piece[0], :, pl.ds(piece[1], piece[2])]
+
+    first = [copy(part_of(own_ref, 0, p), r_one.at[i], r_sems.at[0], i, up) for i, p in enumerate(around)]
+    second = [copy(r_one.at[i], r_two.at[i], r_sems.at[1], i, up) for i, p in enumerate(around)]
+    third = [
+        copy(r_two.at[i], part_of(own_ref, lon_dev, p), r_sems.at[2], i, last) for i, p in enumerate(around)
+    ]
+    e_copies = [
+        copy(part_of(own_ref, 0, p), part_of(own_ref, lon_dev, p), e_sems, i, west) for i, p in enumerate(direct)
+    ]
+    for one in first + e_copies:
         one.start()
     half = lon_dev // 2
     n_copies = [
@@ -103,7 +125,8 @@
         for h in range(2)
     ]
     c_copies = [
-        copy(own_ref.at[lon_dev + j], next_ref.at[lon_dev + j], c_sems, j, south) for j in range(margin)
+        copy(part_of(own_ref, lon_dev, p), part_of(next_ref, lon_dev, p), c_sems, i, south)
+        for i, p in enumerate(direct + around)
     ]
 
     @pl.when(lat > 0)
@@ -115,12 +138,15 @@
     def _():
         next_ref[...] = jnp.zeros_like(next_ref)
 
-    for j in range(margin):
-        e_copies[j].wait_recv()
+    for came, onward in zip(first + second, second + third):
+        came.wait_recv()
+        onward.start()
+    for i, one in enumerate(e_copies + third):
+        one.wait_recv()
 
         @pl.when(lat > 0)
         def _():
-            c_copies[j].start()
+            c_copies[i].start()
 
     @pl.when(lat < n_lat - 1)
     def _():
@@ -132,51 +158,18 @@
         for one in n_copies + c_copies:
             one.wait_send()
 
-    for one in o_copies + e_copies:
+    for one in o_copies + e_copies + first + second + third:
         one.wait_send()
     for one in loads[4:]:
         one.wait()
 
 
-def run_exchange(count, arrays, n_lat, n_x, n_h, n_col, col_rows):
-    tokens, obs, lats, cells = arrays[:4]
-    d_model = obs.shape[1]
-    margin = WIN - 1
-    vmem = pl.BlockSpec(memory_space=pltpu.VMEM)
-    bf16 = jnp.bfloat16
-    block = jax.ShapeDtypeStruct((n_col, col_rows, d_model), bf16)
-    return pl.pallas_call(
-        functools.partial(exchange_kernel, n_x, n_h),
-        out_shape=[block, block] + [jax.ShapeDtypeStruct(one.shape, one.dtype) for one in arrays[4:]],
-        in_specs=[pl.BlockSpec(memory_space=pltpu.SMEM)] + [pl.BlockSpec(memory_space=pltpu.HBM)] * len(arrays),
-        out_specs=[vmem] * (len(arrays) - 2),
-        scratch_shapes=[
-            pltpu.VMEM(tokens.shape, bf16),
-            pltpu.VMEM(obs.shape, bf16),
-            pltpu.VMEM(lats.shape, jnp.int32),
-            pltpu.VMEM(cells.shape, jnp.int32),
-            pltpu.VMEM((n_lat, 8, d_model), bf16),
-            pltpu.VMEM((n_lat, 8, d_model), bf16),
-            pltpu.SemaphoreType.DMA((len(arrays),)),
-            pltpu.SemaphoreType.DMA((2, n_lat - 1)),
-            pltpu.SemaphoreType.DMA((2, margin)),
-            pltpu.SemaphoreType.DMA((2, 2)),
-            pltpu.SemaphoreType.DMA((2, margin)),
-        ],
-        compiler_params=pltpu.CompilerParams(
-            collective_id=1, has_side_effects=True, vmem_limit_bytes=32 << 20
-        ),
-        cost_estimate=pl.CostEstimate(flops=1 << 28, bytes_accessed=80 << 20, transcendentals=0),
-        name="exchange",
-    )(count, *[pltpu.with_memory_space_constraint(one, pltpu.HBM) for one in arrays])
-
-
-def block_kernel(
+def block_part(
     lat_dev, shift_ref, own_ref, next_ref, gain_ref, w_qkv_ref, w_out_ref, cot_ref, out_ref, g_ref,
     region_ref, qkv_ref, ctx_ref, ctx_t_ref,
 ):
     n_tok, d_model = region_ref.shape
-    n_src = own_ref.shape[0]
+    n_src = own_ref.shape[0] * own_ref.shape[1]
     lon_dev = 2 * WIN
     col_rows = n_tok // lon_dev
     lat_shift, lon_shift = shift_ref[0, 0], shift_ref[0, 1]
@@ -189,8 +182,8 @@
     here = jnp.where((source == 0) & (row < lat_dev), 1.0, 0.0).astype(jnp.bfloat16)
     after = jnp.where((source == lat_dev) & (row >= lat_dev), 1.0, 0.0)
     after = jnp.where(row + lax.axis_index("lat") * lat_dev < limit, after, 0.0).astype(jnp.bfloat16)
-    region_ref[...] = jnp.dot(here, own_ref[...], preferred_element_type=jnp.float32) + jnp.dot(
-        after, next_ref[...], preferred_element_type=jnp.float32
+    region_ref[...] = jnp.dot(here, own_ref[...].reshape(n_src, d_model), preferred_element_type=jnp.float32) + jnp.dot(
+        after, next_ref[...].reshape(n_src, d_model), preferred_element_type=jnp.float32
     )
     head_dim = d_model // HEADS
     pair = 2 * head_dim
@@ -249,35 +242,12 @@
                     g_ref[core, x, y, z * 16 : (z + 1) * 16, :] = part[at : at + 16, :]
 
 
-def run_block(lat_dev, shift, own, after, gain, w_qkv, w_out, cot, dims):
-    n_tok, d_model = cot.shape
-    vmem = pl.BlockSpec(memory_space=pltpu.VMEM)
-    return pl.pallas_call(
-        functools.partial(block_kernel, lat_dev),
-        out_shape=(
-            jax.ShapeDtypeStruct((n_tok, d_model), jnp.bfloat16),
-            jax.ShapeDtypeStruct(dims, jnp.bfloat16),
-        ),
-        in_specs=[pl.BlockSpec(memory_space=pltpu.SMEM)] + [vmem] * 6,
-        out_specs=(vmem, vmem),
-        scratch_shapes=[
-            pltpu.VMEM((n_tok, d_model), jnp.float32),
-            pltpu.VMEM((2, n_tok // 2, 3 * d_model), jnp.bfloat16),
-            pltpu.VMEM((n_tok // (2 * WIN), 2, WIN, d_model), jnp.float32),
-            pltpu.VMEM((d_model, n_tok), jnp.bfloat16),
-        ],
-        compiler_params=pltpu.CompilerParams(vmem_limit_bytes=40 << 20),
-        cost_estimate=pl.CostEstimate(flops=3 << 30, bytes_accessed=12 << 20, transcendentals=1 << 19),
-        name="block",
-    )(shift, own, after, gain, w_qkv, w_out, cot)
-
-
-def reduce_kernel(
+def reduce_part(
     n_x, n_y, n_h, n_l,
     g_ref, out_ref,
     c_recv_a, c_recv_b, x_send, x_recv, x_sum, y_send, y_recv, y_sum,
-    a_send, a_recv, b_send, b_recv, l_send, l_recv, h_send, h_recv, t_send, t_recv,
-    c_sems, x_sems, y_sems, a_sems, b_sems, l_sems, h_sems,
+    a_send, a_recv, b_send, b_recv, z_own, z_send, z_recv,
+    c_sems, x_sems, y_sems, a_sems, b_sems, z_sems,
 ):
     lon, lat, y = lax.axis_index("lon"), lax.axis_index("lat"), lax.axis_index("dp")
     x, z_hi = lon // n_h, lon % n_h
@@ -290,21 +260,7 @@
     def at_y(k):
         return {"dp": (y + k) % n_y}
 
-    def at_l(k):
-        return {"lat": ((z_lo + k) % n_l) * 2 + core}
-
-    def at_h(other):
-        return {"lon": x * n_h + other}
-
     pal = {"lat": z_lo * 2 + 1 - core}
-    near = z_hi + 1 - 2 * (z_hi % 2)
-    far = (z_hi + n_h - 1 + 2 * (z_hi % 2)) % n_h
-    peers = [pal] + [at_x(k) for k in range(1, n_x)] + [at_y(k) for k in range(1, n_y)]
-    peers += [at_l(k) for k in range(1, n_l)] + [at_h(near), at_h(far)]
-    barrier = pltpu.get_barrier_semaphore()
-    for peer in peers:
-        pl.semaphore_signal(barrier, inc=1, device_id=peer, device_id_type=MESH)
-    pl.semaphore_wait(barrier, len(peers))
     copies = []
 
     def send(src, dst, sems, k, where):
@@ -375,48 +331,95 @@
     for k in range(1, n_x):
         b_c[k].wait_recv()
         part_b = part_b + b_recv[k - 1].astype(f32)
-    x_sum[0] = part_a
-    x_sum[1] = part_b
     each = rows // n_l
-    l_send[: n_l // 2] = part_a.reshape(n_l // 2, each, wide).astype(bf16)
-    l_send[n_l // 2 :] = part_b.reshape(n_l // 2, each, wide).astype(bf16)
-    l_c = {}
-    for k in range(1, n_l):
-        l_c[k] = send(l_send.at[(z_lo + k) % n_l], l_recv.at[k - 1], l_sems, k - 1, at_l(k))
-    mine = pl.ds(pl.multiple_of((z_lo % (n_l // 2)) * each, each), each)
-    part = x_sum[z_lo // (n_l // 2), mine, :]
-    for k in range(1, n_l):
-        l_c[k].wait_recv()
-        part = part + l_recv[k - 1].astype(f32)
-    h_send[...] = part.astype(bf16)
-    first = send(h_send, h_recv, h_sems, 0, at_h(near))
-    first.wait_recv()
-    part = part + h_recv[...].astype(f32)
-    tile = wide // 2
-    left, right = part[:, :tile], part[:, tile:]
-    t_send[...] = jnp.where(far // 2 == 0, left, right)
-    second = send(t_send, t_recv, h_sems, 1, at_h(far))
-    part = jnp.where(z_hi // 2 == 0, left, right)
-    second.wait_recv()
-    part = part + t_recv[...]
-    out_ref[...] = jnp.where(z_hi % 2 == 0, part[:, : tile // 2], part[:, tile // 2 :])
+    span = wide // n_h
+    for place, whole in ((0, part_a), (n_l // 2, part_b)):
+        for i in range(n_l // 2):
+            for j in range(n_h):
+                tile = whole[i * each : (i + 1) * each, j * span : (j + 1) * span]
+                z_own[place + i, j] = jnp.concatenate([tile[: each // 2], tile[each // 2 :]], axis=1)
+    z_send[...] = z_own[...].astype(bf16)
+    z_c = []
+    for a in (2, 1, 3, 0):
+        for b in (4, 3, 5, 2, 6, 1, 7, 0):
+            if a or b:
+                z_to, l_to = (z_hi + a) % n_h, (z_lo + b) % n_l
+                at = {"lon": x * n_h + z_to, "lat": l_to * 2 + core}
+                k = a * n_l + b - 1
+                z_c.append((k, send(z_send.at[l_to, z_to], z_recv.at[k], z_sems, k, at)))
+    part = z_own[z_lo, z_hi]
+    for k, one in reversed(z_c):
+        one.wait_recv()
+        part = part + z_recv[k].astype(f32)
+    out_ref[: each // 2] = part[:, :span]
+    out_ref[each // 2 :] = part[:, span:]
     for one in copies:
         one.wait_send()
 
 
-def run_reduce(g, n_h):
-    _, n_x, n_y, rows, wide = g.shape
-    n_l = rows // 16
+def whole_kernel(lat_dev, n_x, n_y, n_h, n_l, count_ref, shift_ref, *refs):
+    loaded, refs = refs[:8], refs[8:]
+    (out_ref, grad_ref), refs = refs[:2], refs[2:]
+    (own_ref, next_ref), held, refs = refs[:2], refs[2:6], refs[6:]
+    moved, refs = refs[:14], refs[14:]
+    g_ref, (region_ref, qkv_ref, ctx_ref, ctx_t_ref), refs = refs[0], refs[1:5], refs[5:]
+    lon, y = lax.axis_index("lon"), lax.axis_index("dp")
+    x, z_hi = lon // n_h, lon % n_h
+    peers = [{"lon": ((x + k) % n_x) * n_h + z_hi} for k in range(1, n_x)]
+    peers += [{"dp": (y + k) % n_y} for k in range(1, n_y)]
+    peers += [{"lon": x * n_h + (z_hi + k) % n_h} for k in (1, n_h - 1)]
+    exchange_part(n_x, n_h, peers, count_ref, *loaded, own_ref, next_ref, *held, *moved)
+    gain_ref, w_qkv_ref, w_out_ref, cot_ref = held
+    block_part(
+        lat_dev, shift_ref, own_ref, next_ref, gain_ref, w_qkv_ref, w_out_ref, cot_ref, out_ref, g_ref,
+        region_ref, qkv_ref, ctx_ref, ctx_t_ref,
+    )
+    reduce_part(n_x, n_y, n_h, n_l, g_ref, grad_ref, *refs)
+
+
+def run_whole(count, shift, arrays, lat_dev, n_lat, n_x, n_y, n_h):
+    tokens, obs, lats, cells = arrays[:4]
+    n_tok, d_model = tokens.shape
+    margin = WIN - 1
+    n_col, col_rows = 2 * WIN + margin, n_tok // (2 * WIN)
+    n_l = n_lat // 2
+    rows, wide = d_model // (2 * n_y), d_model // n_x
     half = rows // 2
     vmem = pl.BlockSpec(memory_space=pltpu.VMEM)
+    smem = pl.BlockSpec(memory_space=pltpu.SMEM)
     bf16, f32 = jnp.bfloat16, jnp.float32
     sems = pltpu.SemaphoreType.DMA
+    like = [pltpu.VMEM(one.shape, one.dtype) for one in arrays]
     return pl.pallas_call(
-        functools.partial(reduce_kernel, n_x, n_y, n_h, n_l),
-        out_shape=jax.ShapeDtypeStruct((16, wide // n_h), f32),
-        in_specs=[vmem],
-        out_specs=vmem,
+        functools.partial(whole_kernel, lat_dev, n_x, n_y, n_h, n_l),
+        out_shape=[
+            jax.ShapeDtypeStruct((n_tok, d_model), bf16),
+            jax.ShapeDtypeStruct((16, wide // n_h), f32),
+        ],
+        in_specs=[smem, smem] + [pl.BlockSpec(memory_space=pltpu.HBM)] * len(arrays),
+        out_specs=[vmem, vmem],
         scratch_shapes=[
+            pltpu.VMEM((n_col, col_rows, d_model), bf16),
+            pltpu.VMEM((n_col, col_rows, d_model), bf16),
+        ]
+        + like[4:]
+        + like[:4]
+        + [
+            pltpu.VMEM((n_lat, 8, d_model), bf16),
+            pltpu.VMEM((n_lat, 8, d_model), bf16),
+            pltpu.VMEM((3, col_rows, d_model // 2), bf16),
+            pltpu.VMEM((3, col_rows, d_model // 2), bf16),
+            sems((len(arrays),)),
+            sems((2, n_lat - 1)),
+            sems((2, margin - 1)),
+            sems((2, 2)),
+            sems((2, margin + 2)),
+            sems((3, 2, 3)),
+            pltpu.VMEM((2, n_x, n_y, rows, wide), bf16),
+            pltpu.VMEM((n_tok, d_model), f32),
+            pltpu.VMEM((2, n_tok // 2, 3 * d_model), bf16),
+            pltpu.VMEM((n_tok // (2 * WIN), 2, WIN, d_model), f32),
+            pltpu.VMEM((d_model, n_tok), bf16),
             pltpu.VMEM((n_x, n_y, half, wide), bf16),
             pltpu.VMEM((n_y, n_x, half, wide), bf16),
             pltpu.VMEM((n_x - 1, n_y, half, wide), bf16),
@@ -429,25 +432,21 @@
             pltpu.VMEM((n_y - 1, half, wide), bf16),
             pltpu.VMEM((n_x - 1, half, wide), bf16),
             pltpu.VMEM((n_x - 1, half, wide), bf16),
-            pltpu.VMEM((n_l, 16, wide), bf16),
-            pltpu.VMEM((n_l - 1, 16, wide), bf16),
-            pltpu.VMEM((16, wide), bf16),
-            pltpu.VMEM((16, wide), bf16),
-            pltpu.VMEM((16, wide // 2), f32),
-            pltpu.VMEM((16, wide // 2), f32),
+            pltpu.VMEM((n_l, n_h, 8, wide // 2), f32),
+            pltpu.VMEM((n_l, n_h, 8, wide // 2), bf16),
+            pltpu.VMEM((n_l * n_h - 1, 8, wide // 2), bf16),
             sems((2, 2 * n_x)),
             sems((2, n_x - 1)),
             sems((2, n_y - 1)),
             sems((2, n_y - 1)),
             sems((2, n_x - 1)),
-            sems((2, n_l - 1)),
-            sems((2, 2)),
+            sems((2, n_l * n_h - 1)),
         ],
         compiler_params=pltpu.CompilerParams(
-            collective_id=0, has_side_effects=True, vmem_limit_bytes=24 << 20
+            collective_id=0, has_side_effects=True, vmem_limit_bytes=56 << 20
         ),
-        name="reduce",
-    )(g)
+        name="whole",
+    )(count, shift, *[pltpu.with_memory_space_constraint(one, pltpu.HBM) for one in arrays])
 
 
 def on_device(
@@ -468,7 +467,6 @@
     n_hi = 4
     n_x = lax.axis_size("lon") // n_hi
     n_obs = obs_vectors.shape[0]
-    n_col = lon_dev + WIN - 1
     arrays = (
         tokens.reshape(-1, d_model),
         obs_vectors,
@@ -479,23 +477,8 @@
         w_out,
         cotangent.reshape(-1, d_model),
     )
-    own, after, gain, w_qkv, w_out, cot = run_exchange(
-        obs_count, arrays, n_lat, n_x, n_hi, n_col, levels * lat_dev
-    )
-    mixed, partial_sums = run_block(
-        lat_dev,
-        shift_offsets,
-        own.reshape(-1, d_model),
-        after.reshape(-1, d_model),
-        gain,
-        w_qkv,
-        w_out,
-        cot,
-        (2, n_x, n_dp, d_model // (2 * n_dp), d_model // n_x),
-    )
-    reduced = run_reduce(partial_sums, n_hi)
-    gradient = reduced.T
-    return (mixed.reshape(tokens.shape), gradient)
+    mixed, gradient = run_whole(obs_count, shift_offsets, arrays, lat_dev, n_lat, n_x, n_dp, n_hi)
+    return (mixed.reshape(tokens.shape), gradient.T)
 
 
 def solution(mesh):

time: 134 us -> 117 us (0.87); the launches traced: 132 us -> 117 us
  Pallas kernels: 130 us -> 113 us
  local copies, waits for them, and re-layouts: 0.61 us -> 3.18 us
    pallas_call x3 -> x1, Pallas kernels: 130 us -> 113 us  [run_whole(): pl.pallas_call(functools.partial(whole_kernel, lat_dev, n_x, n_y, n_h, n_...]
    unnamed x3 -> x2, local copies, waits for them, and re-layouts: 0.61 us -> 3.18 us
where the time goes in v3:
time: 117 us
  Pallas kernels  113 us (97%)
  local copies, waits for them, and re-layouts  3.18 us (3%)
  between operations  1.29 us (1%)
    pallas_call x1, Pallas kernels, run_whole(): pl.pallas_call(functools.partial(whole_kernel, lat_dev, n_x, n_y, n_h, n_...  113 us
    unnamed x2, local copies, waits for them, and re-layouts  3.18 us

profile of v3, /device:TPU:1, one launch (start us, length us, event | category | flops | bytes accessed | tf_op | source)
XLA Modules:
  0.0 117.1 jit_solution(3460230308269727436)
XLA Ops:
  1.3 112.6 %whole.1 = (bf16[256,1024]{1,0:T(8,128)(2,1)}, f32[16,64]{1,0:T(8,128)}) custom-call(s32[1]{0:T(128)S(6)} %copy.14.count_ref, s32[1,2]{1,0:T(1,128)} %shift_ref.1, bf16[256,1024]{1,0:T(8,128)(2,1)} %bitcast.7, bf16[64,1024]{1,0:T(8,128)(2,1)} %refs_1_.1, s32[1,64]{1,0:T(1,128)} %bitcast.12, s32[1,64]{1,0:T(1,128)} %bitcast.13, f32[1,1024]{1,0:T(1,128)} %bitcast.11, ...), custom_call_target="tpu_custom_call" | custom-call | tf_op jit(solution)/shard_map/whole/pallas_call | solution.py:393
  113.9 1.9 %copy.15 = bf16[1,2,8,16,1024]{4,3,2,1,0:T(8,128)(2,1)} copy(bf16[1,2,8,16,1024]{4,3,2,1,0:T(8,128)(2,1)} %bitcast.9) | data formatting | bytes 1048576
  115.8 1.3 %copy.16 = f32[64,16]{0,1:T(8,128)} copy(f32[64,16]{0,1:T(8,128)} %bitcast.10) | data formatting | bytes 8192

commit v4 on v3

--- a/solution.py
+++ b/solution.py
@@ -17,7 +17,7 @@
     count_ref, tok_hbm, obs_hbm, lat_hbm, cell_hbm, gain_hbm, w_qkv_hbm, w_out_hbm, cot_hbm,
     own_ref, next_ref, gain_ref, w_qkv_ref, w_out_ref, cot_ref,
     tok_ref, obs_ref, lat_ref, cell_ref, send, recv, r_one, r_two,
-    l_sems, o_sems, e_sems, n_sems, c_sems, r_sems,
+    l_sems, o_sems, e_sems, n_sems, c_sems, r_sems, cot_pal_ref, s_sems,
 ):
     loads = []
     for src, dst in (
@@ -53,14 +53,25 @@
     bound = lat_ref[...] == slot // 8
     earlier = lax.broadcasted_iota(i32, (n_obs, n_obs), 0) < lax.broadcasted_iota(i32, (n_obs, n_obs), 1)
     rank = jnp.dot(bound.astype(f32).astype(bf16), earlier.astype(f32).astype(bf16), preferred_element_type=f32)
-    chooser = jnp.where(bound & (rank == (slot % 8).astype(f32)), 1.0, 0.0).astype(bf16)
-    rows = jnp.dot(chooser, obs_ref[...], preferred_element_type=f32).reshape(n_lat, 8, d_model)
+    quarter = d_model // 4
+    seat = slot % 8
+
+    def chosen(wanted):
+        return jnp.where(bound & (rank == wanted.astype(f32)), 1.0, 0.0).astype(bf16)
+
+    chooser = chosen(seat)
+    last_part = obs_ref[:, 3 * quarter :]
     live = lax.broadcasted_iota(i32, (8, n_obs), 1) < count_ref[0]
     tags = jnp.where(live, cell_ref[...] + 1, 0).astype(f32).astype(bf16)
     tags = lax.dot_general(tags, chooser, (((1,), (1,)), ((), ())), preferred_element_type=f32)
     at_tag = lax.broadcasted_iota(i32, (n_lat, 8, n_slots), 1) == 6
-    send[:, :, :n_slots] = jnp.where(at_tag, tags[None], rows[:, :, :n_slots]).astype(bf16)
-    send[:, :, n_slots:] = rows[:, :, n_slots:].astype(bf16)
+    send[:, :, 3 * quarter :] = jnp.where(at_tag, tags[None], 0.0).astype(bf16)
+    for j in range(3):
+        cols = slice(j * quarter, (j + 1) * quarter)
+        rows = jnp.dot(chooser, obs_ref[:, cols], preferred_element_type=f32)
+        extra = chosen(jnp.where(seat < 6, -1, (seat - 6) * 3 + j))
+        rows = rows + jnp.dot(extra, last_part, preferred_element_type=f32)
+        send[:, :, cols] = rows.reshape(n_lat, 8, quarter).astype(bf16)
     recv[lat] = send[lat]
 
     pl.semaphore_wait(barrier, len(peers))
@@ -76,6 +87,8 @@
     ]
     for one in o_copies:
         one.start()
+    swap = copy(cot_hbm, cot_pal_ref, s_sems, 0, {"lat": lat + 1 - 2 * (lat % 2)})
+    swap.start()
     loads[3].wait()
     n_col, col_rows, _ = own_ref.shape
     lon_dev = tok_ref.shape[0] // col_rows
@@ -88,18 +101,24 @@
     for one in o_copies:
         one.wait_recv()
     got = recv[...].astype(f32)
-    slots = got[:, :, :n_slots]
+    slots = got[:, :, 3 * quarter :]
     sub = lax.broadcasted_iota(i32, slots.shape, 1)
     tag = jnp.sum(jnp.where(sub == 6, slots, 0.0), axis=1, keepdims=True)
-    lane = lax.broadcasted_iota(i32, slots.shape, 2)
-    tag = jnp.sum(jnp.where(lane == lat * 8 + sub, tag, 0.0), axis=2, keepdims=True)
-    tag = tag.reshape(n_slots, 1)
+    lane = lax.broadcasted_iota(i32, slots.shape, 2) - lat * 8
     place = lax.broadcasted_iota(i32, (n_slots, n_tok), 1)
     cell = (place % col_rows) * lon_dev + place // col_rows + 1
-    placer = jnp.where(tag == cell.astype(f32), 1.0, 0.0).astype(bf16)
-    added = lax.dot_general(
-        placer, got.reshape(n_slots, d_model).astype(bf16), (((0,), (0,)), ((), ())), preferred_element_type=f32
-    )
+    got = got.reshape(n_slots, 3 * quarter + n_slots).astype(bf16)
+
+    def placed(wanted, cols):
+        mine = jnp.sum(jnp.where(lane == wanted, tag, 0.0), axis=2, keepdims=True).reshape(n_slots, 1)
+        placer = jnp.where(mine == cell.astype(f32), 1.0, 0.0).astype(bf16)
+        return lax.dot_general(placer, got[:, cols], (((0,), (0,)), ((), ())), preferred_element_type=f32)
+
+    added = [placed(sub, slice(0, 3 * quarter)), 0.0]
+    for j in range(3):
+        wanted = jnp.where(sub < 6, -1 - lat * 8, (sub - 6) * 3 + j)
+        added[1] = added[1] + placed(wanted, slice(j * quarter, (j + 1) * quarter))
+    added = jnp.concatenate(added, axis=1)
     own_ref[:lon_dev] = (turned + added).astype(bf16).reshape(lon_dev, col_rows, d_model)
 
     wide = d_model // 2
@@ -162,11 +181,12 @@
         one.wait_send()
     for one in loads[4:]:
         one.wait()
+    swap.wait()
 
 
 def block_part(
-    lat_dev, shift_ref, own_ref, next_ref, gain_ref, w_qkv_ref, w_out_ref, cot_ref, out_ref, g_ref,
-    region_ref, qkv_ref, ctx_ref, ctx_t_ref,
+    lat_dev, shift_ref, own_ref, next_ref, gain_ref, w_qkv_ref, w_out_ref, out_ref,
+    region_ref, qkv_ref, ctx_ref, ctx_t_ref, ctx_pal_ref, s_sems,
 ):
     n_tok, d_model = region_ref.shape
     n_src = own_ref.shape[0] * own_ref.shape[1]
@@ -225,29 +245,24 @@
             context = jnp.dot(jnp.concatenate(weights, axis=1), values, preferred_element_type=jnp.float32)
             ctx_ref[:, win, :, at : at + pair] = context.reshape(groups, WIN, pair)
     context = ctx_ref[...].reshape(n_tok, d_model).astype(jnp.bfloat16)
+    ctx_t_ref[...] = context.T.reshape(ctx_t_ref.shape)
+    lat = lax.axis_index("lat")
+    swap = pltpu.make_async_remote_copy(
+        src_ref=ctx_t_ref.at[:, 1 - lat % 2], dst_ref=ctx_pal_ref, send_sem=s_sems.at[0, 1],
+        recv_sem=s_sems.at[1, 1], device_id={"lat": lat + 1 - 2 * (lat % 2)}, device_id_type=MESH,
+    )
+    swap.start()
     for col in range(0, d_model, block):
         result = jnp.dot(context, w_out_ref[:, col : col + block], preferred_element_type=jnp.float32)
         out_ref[:, col : col + block] = (region_ref[:, col : col + block] + result).astype(jnp.bfloat16)
-    ctx_t_ref[...] = context.T
-    cores, n_x, n_y, rows, wide = g_ref.shape
-    n_z = rows // 16
-    for x in range(n_x):
-        part = jnp.dot(
-            ctx_t_ref[...], cot_ref[:, x * wide : (x + 1) * wide], preferred_element_type=jnp.float32
-        ).astype(jnp.bfloat16)
-        for z in range(n_z):
-            for core in range(cores):
-                for y in range(n_y):
-                    at = ((z * cores + core) * n_y + y) * 16
-                    g_ref[core, x, y, z * 16 : (z + 1) * 16, :] = part[at : at + 16, :]
+    swap.wait()
 
 
 def reduce_part(
     n_x, n_y, n_h, n_l,
-    g_ref, out_ref,
-    c_recv_a, c_recv_b, x_send, x_recv, x_sum, y_send, y_recv, y_sum,
-    a_send, a_recv, b_send, b_recv, z_own, z_send, z_recv,
-    c_sems, x_sems, y_sems, a_sems, b_sems, z_sems,
+    ctx_t_ref, ctx_pal_ref, cot_ref, cot_pal_ref, out_ref,
+    x_send, x_recv, x_sum, y_send, y_recv, y_sum, a_send, a_recv, b_send, b_recv, z_own, z_send, z_recv,
+    x_sems, y_sems, a_sems, b_sems, z_sems,
 ):
     lon, lat, y = lax.axis_index("lon"), lax.axis_index("lat"), lax.axis_index("dp")
     x, z_hi = lon // n_h, lon % n_h
@@ -260,7 +275,6 @@
     def at_y(k):
         return {"dp": (y + k) % n_y}
 
-    pal = {"lat": z_lo * 2 + 1 - core}
     copies = []
 
     def send(src, dst, sems, k, where):
@@ -272,38 +286,32 @@
         copies.append(one)
         return one
 
-    _, _, _, rows, wide = g_ref.shape
-    half = rows // 2
-    low, high = pl.ds(0, half), pl.ds(half, half)
+    n_tok, d_model = cot_ref.shape
+    wide = d_model // n_x
+    half = (n_l // 2) * 16
     order = [2, 1, 3, 0]
-    c_a, c_b = {}, {}
-    for i, k in enumerate(order):
-        dest = (x + k) % n_x
-        c_a[k] = send(g_ref.at[1 - core, dest, :, low], c_recv_a.at[k], c_sems, 2 * i, pal)
-        dest = (y + k) % n_y
-        c_b[k] = send(g_ref.at[1 - core, :, dest, high], c_recv_b.at[k], c_sems, 2 * i + 1, pal)
+    mine = ctx_t_ref[:, core].reshape(d_model // 2, n_tok)
+    theirs = ctx_pal_ref[...].reshape(d_model // 2, n_tok)
     x_c, y_c = {}, {}
     for k in order:
-        c_a[k].wait_recv()
         dest = (x + k) % n_x
+        cols = pl.ds(pl.multiple_of(dest * wide, wide), wide)
+        part = jnp.dot(mine, cot_ref[:, cols], preferred_element_type=f32)
+        part = part + jnp.dot(theirs, cot_pal_ref[:, cols], preferred_element_type=f32)
+        part = part.reshape(n_l, n_y, 16, wide)
         for i in range(n_y):
-            part = g_ref[core, dest, i, :half].astype(f32) + c_recv_a[k, i].astype(f32)
+            low = part[: n_l // 2, i].reshape(half, wide)
+            high = part[n_l // 2 :, i].reshape(half, wide)
             if k:
-                x_send[k - 1, i] = part.astype(bf16)
+                x_send[k - 1, i] = low.astype(bf16)
             else:
-                x_sum[i] = part
+                x_sum[i] = low
+            y_sum[i, dest] = high
+            y_send[i, dest] = high.astype(bf16)
         if k:
             x_c[k] = send(x_send.at[k - 1], x_recv.at[k - 1], x_sems, k - 1, at_x(k))
-        c_b[k].wait_recv()
-        dest = (y + k) % n_y
-        for i in range(n_x):
-            part = g_ref[core, i, dest, half:].astype(f32) + c_recv_b[k, i].astype(f32)
-            if k:
-                y_send[k - 1, i] = part.astype(bf16)
-            else:
-                y_sum[i] = part
-        if k:
-            y_c[k] = send(y_send.at[k - 1], y_recv.at[k - 1], y_sems, k - 1, at_y(k))
+    for k in order[:3]:
+        y_c[k] = send(y_send.at[(y + k) % n_y], y_recv.at[k - 1], y_sems, k - 1, at_y(k))
     for k in range(1, n_x):
         x_c[k].wait_recv()
     a_c, b_c = {}, {}
@@ -319,7 +327,7 @@
         y_c[k].wait_recv()
     for k in order:
         dest = (x + k) % n_x
-        part_b = y_sum[dest]
+        part_b = y_sum[y, dest]
         for j in range(n_y - 1):
             part_b = part_b + y_recv[j, dest].astype(f32)
         if k:
@@ -331,7 +339,7 @@
     for k in range(1, n_x):
         b_c[k].wait_recv()
         part_b = part_b + b_recv[k - 1].astype(f32)
-    each = rows // n_l
+    each = 16
     span = wide // n_h
     for place, whole in ((0, part_a), (n_l // 2, part_b)):
         for i in range(n_l // 2):
@@ -362,19 +370,20 @@
     (out_ref, grad_ref), refs = refs[:2], refs[2:]
     (own_ref, next_ref), held, refs = refs[:2], refs[2:6], refs[6:]
     moved, refs = refs[:14], refs[14:]
-    g_ref, (region_ref, qkv_ref, ctx_ref, ctx_t_ref), refs = refs[0], refs[1:5], refs[5:]
+    (cot_pal_ref, s_sems), refs = refs[:2], refs[2:]
+    (region_ref, qkv_ref, ctx_ref, ctx_t_ref, ctx_pal_ref), refs = refs[:5], refs[5:]
     lon, y = lax.axis_index("lon"), lax.axis_index("dp")
     x, z_hi = lon // n_h, lon % n_h
     peers = [{"lon": ((x + k) % n_x) * n_h + z_hi} for k in range(1, n_x)]
     peers += [{"dp": (y + k) % n_y} for k in range(1, n_y)]
     peers += [{"lon": x * n_h + (z_hi + k) % n_h} for k in (1, n_h - 1)]
-    exchange_part(n_x, n_h, peers, count_ref, *loaded, own_ref, next_ref, *held, *moved)
+    exchange_part(n_x, n_h, peers, count_ref, *loaded, own_ref, next_ref, *held, *moved, cot_pal_ref, s_sems)
     gain_ref, w_qkv_ref, w_out_ref, cot_ref = held
     block_part(
-        lat_dev, shift_ref, own_ref, next_ref, gain_ref, w_qkv_ref, w_out_ref, cot_ref, out_ref, g_ref,
-        region_ref, qkv_ref, ctx_ref, ctx_t_ref,
+        lat_dev, shift_ref, own_ref, next_ref, gain_ref, w_qkv_ref, w_out_ref, out_ref,
+        region_ref, qkv_ref, ctx_ref, ctx_t_ref, ctx_pal_ref, s_sems,
     )
-    reduce_part(n_x, n_y, n_h, n_l, g_ref, grad_ref, *refs)
+    reduce_part(n_x, n_y, n_h, n_l, ctx_t_ref, ctx_pal_ref, cot_ref, cot_pal_ref, grad_ref, *refs)
 
 
 def run_whole(count, shift, arrays, lat_dev, n_lat, n_x, n_y, n_h):
@@ -405,8 +414,8 @@
         + like[4:]
         + like[:4]
         + [
-            pltpu.VMEM((n_lat, 8, d_model), bf16),
-            pltpu.VMEM((n_lat, 8, d_model), bf16),
+            pltpu.VMEM((n_lat, 8, d_model - d_model // 4 + n_lat * 8), bf16),
+            pltpu.VMEM((n_lat, 8, d_model - d_model // 4 + n_lat * 8), bf16),
             pltpu.VMEM((3, col_rows, d_model // 2), bf16),
             pltpu.VMEM((3, col_rows, d_model // 2), bf16),
             sems((len(arrays),)),
@@ -415,19 +424,19 @@
             sems((2, 2)),
             sems((2, margin + 2)),
             sems((3, 2, 3)),
-            pltpu.VMEM((2, n_x, n_y, rows, wide), bf16),
+            pltpu.VMEM((n_tok, d_model), bf16),
+            sems((2, 2)),
             pltpu.VMEM((n_tok, d_model), f32),
             pltpu.VMEM((2, n_tok // 2, 3 * d_model), bf16),
             pltpu.VMEM((n_tok // (2 * WIN), 2, WIN, d_model), f32),
-            pltpu.VMEM((d_model, n_tok), bf16),
-            pltpu.VMEM((n_x, n_y, half, wide), bf16),
-            pltpu.VMEM((n_y, n_x, half, wide), bf16),
+            pltpu.VMEM((n_l, 2, rows // 2, n_tok), bf16),
+            pltpu.VMEM((n_l, rows // 2, n_tok), bf16),
             pltpu.VMEM((n_x - 1, n_y, half, wide), bf16),
             pltpu.VMEM((n_x - 1, n_y, half, wide), bf16),
             pltpu.VMEM((n_y, half, wide), f32),
+            pltpu.VMEM((n_y, n_x, half, wide), bf16),
             pltpu.VMEM((n_y - 1, n_x, half, wide), bf16),
-            pltpu.VMEM((n_y - 1, n_x, half, wide), bf16),
-            pltpu.VMEM((n_x, half, wide), f32),
+            pltpu.VMEM((n_y, n_x, half, wide), f32),
             pltpu.VMEM((n_y - 1, half, wide), bf16),
             pltpu.VMEM((n_y - 1, half, wide), bf16),
             pltpu.VMEM((n_x - 1, half, wide), bf16),
@@ -435,7 +444,6 @@
             pltpu.VMEM((n_l, n_h, 8, wide // 2), f32),
             pltpu.VMEM((n_l, n_h, 8, wide // 2), bf16),
             pltpu.VMEM((n_l * n_h - 1, 8, wide // 2), bf16),
-            sems((2, 2 * n_x)),
             sems((2, n_x - 1)),
             sems((2, n_y - 1)),
             sems((2, n_y - 1)),
@@ -443,7 +451,7 @@
             sems((2, n_l * n_h - 1)),
         ],
         compiler_params=pltpu.CompilerParams(
-            collective_id=0, has_side_effects=True, vmem_limit_bytes=56 << 20
+            collective_id=0, has_side_effects=True, vmem_limit_bytes=40 << 20
         ),
         name="whole",
     )(count, shift, *[pltpu.with_memory_space_constraint(one, pltpu.HBM) for one in arrays])

time: 117 us -> 116 us (level)
    unnamed x2 -> x4, local copies, waits for them, and re-layouts: 3.18 us -> 2.04 us
where the time goes in v4:
time: 116 us; the launch traced here: 115 us
  Pallas kernels  112 us (97%)
  local copies, waits for them, and re-layouts  2.04 us (2%)
  between operations  1.3 us (1%)
    pallas_call x1, Pallas kernels, run_whole(): pl.pallas_call(functools.partial(whole_kernel, lat_dev, n_x, n_y, n_h, n_...  112 us

profile of v4, /device:TPU:1, one launch (start us, length us, event | category | flops | bytes accessed | tf_op | source)
XLA Modules:
  0.0 115.3 jit_solution(12321987701528559521)
XLA Ops:
  1.3 0.0 copy-start
  1.3 0.6 copy-done
  1.9 111.9 %whole.1 = (bf16[256,1024]{1,0:T(8,128)(2,1)S(1)}, f32[16,64]{1,0:T(8,128)S(1)}) custom-call(s32[1]{0:T(128)S(6)} %copy.14.count_ref, s32[1,2]{1,0:T(1,128)S(1)} %copy-done, bf16[256,1024]{1,0:T(8,128)(2,1)} %bitcast.9, bf16[64,1024]{1,0:T(8,128)(2,1)} %refs_1_.1, s32[1,64]{1,0:T(1,128)} %bitcast.12, s32[1,64]{1,0:T(1,128)} %bitcast.13, f32[1,1024]{1,0:T(1,128)} %bitcast.11, ...), custom_call_target="tpu_custom_call" | custom-call | tf_op jit(solution)/shard_map/whole/pallas_call | solution.py:402
  113.9 0.8 copy.15
  114.7 0.6 copy.16
Async XLA Ops:
  1.3 0.7 copy-start

commit v5 on v4

--- a/solution.py
+++ b/solution.py
@@ -123,7 +123,9 @@
 
     wide = d_model // 2
     direct = [(j, 0, d_model) for j in range(margin - 2)] + [(margin - 2, 0, wide)]
-    around = [(margin - 2, wide, wide), (margin - 1, 0, wide), (margin - 1, wide, wide)]
+    piece_w = d_model // 4
+    around = [(margin - 2, c * piece_w, piece_w) for c in (2, 3)]
+    around += [(margin - 1, c * piece_w, piece_w) for c in range(4)]
 
     def part_of(ref, col, piece):
         return ref.at[col + piece[0], :, pl.ds(piece[1], piece[2])]
@@ -416,14 +418,14 @@
         + [
             pltpu.VMEM((n_lat, 8, d_model - d_model // 4 + n_lat * 8), bf16),
             pltpu.VMEM((n_lat, 8, d_model - d_model // 4 + n_lat * 8), bf16),
-            pltpu.VMEM((3, col_rows, d_model // 2), bf16),
-            pltpu.VMEM((3, col_rows, d_model // 2), bf16),
+            pltpu.VMEM((6, col_rows, d_model // 4), bf16),
+            pltpu.VMEM((6, col_rows, d_model // 4), bf16),
             sems((len(arrays),)),
             sems((2, n_lat - 1)),
             sems((2, margin - 1)),
             sems((2, 2)),
-            sems((2, margin + 2)),
-            sems((3, 2, 3)),
+            sems((2, margin + 5)),
+            sems((3, 2, 6)),
             pltpu.VMEM((n_tok, d_model), bf16),
             sems((2, 2)),
             pltpu.VMEM((n_tok, d_model), f32),

time: 116 us -> 116 us (level)
  no operation moved by 1% of the time
where the time goes in v5:
time: 116 us
  Pallas kernels  112 us (97%)
  local copies, waits for them, and re-layouts  2.04 us (2%)
  between operations  1.3 us (1%)
    pallas_call x1, Pallas kernels, run_whole(): pl.pallas_call(functools.partial(whole_kernel, lat_dev, n_x, n_y, n_h, n_...  112 us

profile of v5, /device:TPU:1, one launch (start us, length us, event | category | flops | bytes accessed | tf_op | source)
XLA Modules:
  0.0 115.6 jit_solution(14002220690014884002)
XLA Ops:
  1.3 0.0 copy-start
  1.3 0.6 copy-done
  1.9 112.3 %whole.1 = (bf16[256,1024]{1,0:T(8,128)(2,1)S(1)}, f32[16,64]{1,0:T(8,128)S(1)}) custom-call(s32[1]{0:T(128)S(6)} %copy.14.count_ref, s32[1,2]{1,0:T(1,128)S(1)} %copy-done, bf16[256,1024]{1,0:T(8,128)(2,1)} %bitcast.9, bf16[64,1024]{1,0:T(8,128)(2,1)} %refs_1_.1, s32[1,64]{1,0:T(1,128)} %bitcast.12, s32[1,64]{1,0:T(1,128)} %bitcast.13, f32[1,1024]{1,0:T(1,128)} %bitcast.11, ...), custom_call_target="tpu_custom_call" | custom-call | tf_op jit(solution)/shard_map/whole/pallas_call | solution.py:404
  114.2 0.8 copy.15
  115.0 0.6 copy.16
Async XLA Ops:
  1.3 0.7 copy-start
